TPU v7x, 32 devices: a whole 2x2x4 slice. The times are simulated.
32 devices in a mesh: gx: 4 (over y, x), gy: 8 (over z, core).
Axes of the slice: x: 2, y: 2, z: 4, core: 2. Of those that a mesh axis runs over, the one named last changes fastest.
Arguments:
- adjoint_prev: float32 [2, 20, 256, 1024], P(None, None, 'gx', 'gy'), may hold values from -2 to 2
- viscosity: float32 [20, 256, 1024], P(None, 'gx', 'gy'), may hold values from 0.5 to 4
- friction: float32 [256, 1024], P('gx', 'gy'), may hold values from 0.5 to 20
- basal_velocity: float32 [2, 256, 1024], P(None, 'gx', 'gy'), may hold values from -6 to 6
- ice_mask: int32 [256, 1024], P('gx', 'gy'), may hold values 0 or 1
- misfit: bfloat16 [32768, 2, 128], P(('gx', 'gy')), may hold values from -60 to 60
- block_tile: int32 [32768, 1], P(('gx', 'gy')), may hold values from 0 to 31; in each aligned block of 1024 rows (0 to 1023, 1024 to 2047, ...) at most 64 rows name the same one
- block_row: int32 [32768], P(('gx', 'gy')), may hold values from 0 to 63
Outputs:
- adjoint: float32 [2, 20, 256, 1024], P(None, None, 'gx', 'gy')
- gradient: float32 [256, 1024], P('gx', 'gy')
Inputs may be any that keep to these rules, and one draw needn't show every extreme that they name: `block_tile`: among the 1024 blocks of one device no tile is named more than 64 times, a bound that some block reaches.
All inputs are finite; a program needn't handle non-finite values. No bound on the sum of `ice_mask` on one device may be relied on, other than what follows from the above.
Results may differ from a plain program's by a relative error of at most 0.0003.
Values may be sent and summed in bfloat16 or wider, within the bound.
No kernel may reach another device: no remote copies, remote signals or barrier semaphores. Data moves between devices by JAX's collectives and lax.ppermute only.
A program may use at most 64 MiB of HBM per device.

v0:
```python
import math

import jax
import jax.numpy as jnp
from jax import lax
from jax.sharding import PartitionSpec as P

ITERS = 3


VERTICAL = 4.0


def with_halo(array, sides, width):
    for axis, dim in sides:
        peers, length = (lax.axis_size(axis), array.shape[dim])
        up = [(i, (i + 1) % peers) for i in range(peers - 1)]
        down = [(j, i) for i, j in up]
        last = lax.slice_in_dim(array, length - width, length, axis=dim)
        initial = lax.slice_in_dim(array, 0, width, axis=dim)
        before = lax.ppermute(last, axis, up)
        after = lax.ppermute(initial, axis, down)
        array = jnp.concatenate([before, array, after], axis=dim)
    return array


def omega_list(count):
    return [
        1.0 / (1.3 + 1.2 * math.cos((2 * turn_id + 1) * math.pi / (2 * count)))
        for turn_id in range(count)
    ]


def coefficients(padded_eta, friction):
    center = padded_eta[:, 1:-1, 1:-1]
    x_low = 0.5 * (padded_eta[:, :-2, 1:-1] + center)
    x_high = 0.5 * (padded_eta[:, 2:, 1:-1] + center)
    y_low = 0.5 * (padded_eta[:, 1:-1, :-2] + center)
    y_high = 0.5 * (padded_eta[:, 1:-1, 2:] + center)
    layer_face = 0.5 * (center[:-1] + center[1:])
    zero_face = jnp.zeros_like(center[:1])
    z_up = jnp.concatenate([zero_face, layer_face], axis=0)
    z_down = jnp.concatenate([layer_face, zero_face], axis=0)
    basal = jnp.concatenate([jnp.zeros_like(center[:-1]), friction[None]], axis=0)
    horiz_x = x_low + x_high
    horiz_y = y_low + y_high
    vertical = VERTICAL * (z_up + z_down) + basal
    diagonal = jnp.stack([4.0 * horiz_x + horiz_y + vertical, horiz_x + 4.0 * horiz_y + vertical])
    return ((x_low, x_high, y_low, y_high, z_up, z_down, basal), diagonal)


def diffuse(padded, coeff, weight_x, weight_y):
    x_low, x_high, y_low, y_high, z_up, z_down, basal = coeff
    center = padded[:, 1:-1, 1:-1]
    zero_layer = jnp.zeros_like(center[:1])
    above = jnp.concatenate([zero_layer, center[:-1]], axis=0)
    below = jnp.concatenate([center[1:], zero_layer], axis=0)
    total = weight_x * (
        x_low * (center - padded[:, :-2, 1:-1]) + x_high * (center - padded[:, 2:, 1:-1])
    )
    total = total + weight_y * (
        y_low * (center - padded[:, 1:-1, :-2]) + y_high * (center - padded[:, 1:-1, 2:])
    )
    total = total + VERTICAL * (z_up * (center - above) + z_down * (center - below))
    return total + basal * center


def mixed(padded, padded_eta, weight_x, weight_y):
    along_y = 0.5 * (padded[:, :, 2:] - padded[:, :, :-2])
    flux_x = weight_x * padded_eta[:, :, 1:-1] * along_y
    along_x = 0.5 * (padded[:, 2:, :] - padded[:, :-2, :])
    flux_y = weight_y * padded_eta[:, 1:-1, :] * along_x
    return -(0.5 * (flux_x[:, 2:] - flux_x[:, :-2]) + 0.5 * (flux_y[:, :, 2:] - flux_y[:, :, :-2]))


def operate(padded_adj, padded_eta, coeff):
    first = diffuse(padded_adj[0], coeff, 4.0, 1.0) + mixed(padded_adj[1], padded_eta, 2.0, 1.0)
    second = diffuse(padded_adj[1], coeff, 1.0, 4.0) + mixed(padded_adj[0], padded_eta, 1.0, 2.0)
    return jnp.stack([first, second])


def extend(stacked):
    return with_halo(stacked, (("gx", 1), ("gy", 2)), 1)


def on_device(
    adjoint_prev, viscosity, friction, basal_velocity, ice_mask, misfit, block_tile, block_row
):
    count_x = lax.axis_size("gx")
    count_y = lax.axis_size("gy")
    device_count = count_x * count_y
    block_count = misfit.shape[0]
    tile_cols = misfit.shape[2]
    capacity = 2 * block_count // device_count
    layer_count = adjoint_prev.shape[1]
    tile_rows = adjoint_prev.shape[2]
    target = block_tile[:, 0]
    onehot = (target[:, None] == jnp.arange(device_count, dtype=jnp.int32)[None, :]).astype(
        jnp.int32
    )
    before = jnp.cumsum(onehot, axis=0) - onehot
    position = jnp.sum(before * onehot, axis=1)
    slot_id = target * capacity + position
    slot_total = device_count * capacity
    slot_block = math.gcd(slot_total, 512)
    flat_misfit = misfit.reshape(block_count, 2 * tile_cols)

    def pack_slots(first_slot):
        wanted = first_slot + jnp.arange(slot_block, dtype=jnp.int32)
        select = wanted[:, None] == slot_id[None, :]
        picked = jnp.dot(
            select.astype(jnp.bfloat16), flat_misfit, preferred_element_type=jnp.float32
        )
        filled = jnp.any(select, axis=1)
        rows_here = jnp.sum(jnp.where(select, block_row[None, :], 0), axis=1)
        rows_here = jnp.where(filled, rows_here, -1)
        return (picked.astype(jnp.bfloat16), rows_here)

    starts = jnp.arange(slot_total // slot_block, dtype=jnp.int32) * slot_block
    packed_values, packed_rows = lax.map(pack_slots, starts)
    send_values = packed_values.reshape(slot_total, 2, tile_cols)
    send_rows = packed_rows.reshape(slot_total)
    got_values, got_rows = (
        lax.all_to_all(
            send_values.reshape(device_count, capacity, 2, tile_cols),
            ("gx", "gy"),
            split_axis=0,
            concat_axis=0,
            tiled=True,
        ),
        lax.all_to_all(
            send_rows.reshape(device_count, capacity),
            ("gx", "gy"),
            split_axis=0,
            concat_axis=0,
            tiled=True,
        ),
    )
    got_values = got_values.reshape(device_count * capacity, 2, tile_cols)
    got_rows = got_rows.reshape(device_count * capacity)
    row_table = (got_rows[:, None] == jnp.arange(tile_rows, dtype=jnp.int32)[None, :]).astype(
        jnp.bfloat16
    )
    surface = jnp.einsum("rx,rcy->cxy", row_table, got_values, preferred_element_type=jnp.float32)
    ice = ice_mask.astype(jnp.float32)
    adjoint = ice * adjoint_prev
    source = jnp.zeros(adjoint_prev.shape, jnp.float32).at[:, 0].set(surface)
    padded_eta = None
    coeff = None
    diagonal = None
    for turn_id, omega in enumerate(omega_list(ITERS)):
        flat_adjoint = adjoint.reshape(2 * layer_count, tile_rows, tile_cols)
        if turn_id == 0:
            padded = extend(jnp.concatenate([flat_adjoint, viscosity], axis=0))
            padded_adj = padded[: 2 * layer_count]
            padded_eta = padded[2 * layer_count :]
            coeff, diagonal = coefficients(padded_eta, friction)
        else:
            padded_adj = extend(flat_adjoint)
        padded_adj = padded_adj.reshape(2, layer_count, tile_rows + 2, tile_cols + 2)
        image = operate(padded_adj, padded_eta, coeff)
        adjoint = ice * (adjoint + omega * (source - image) / diagonal)
    gradient = (
        -friction
        * ice
        * (
            basal_velocity[0] * adjoint[0, layer_count - 1]
            + basal_velocity[1] * adjoint[1, layer_count - 1]
        )
    )
    return (adjoint, gradient)


def solution(mesh):
    placed = (
        P(None, None, "gx", "gy"),
        P(None, "gx", "gy"),
        P("gx", "gy"),
        P(None, "gx", "gy"),
        P("gx", "gy"),
        P(("gx", "gy"), None, None),
        P(("gx", "gy"), None),
        P(("gx", "gy")),
    )
    return jax.shard_map(
        on_device,
        mesh=mesh,
        in_specs=placed,
        out_specs=(P(None, None, "gx", "gy"), P("gx", "gy")),
        check_vma=False,
    )
```

profile of v0, /device:TPU:1, one launch (start us, length us, event | category | flops | bytes accessed | tf_op | source)
XLA Modules:
  0.0 175.3 jit_solution(11054078830842546426)
XLA Ops:
  1.4 1.5 broadcast_multiply_fusion
  3.0 4.1 %collective-permute-start = (f32[60,1,128]{2,1,0:T(1,128)S(1)}, f32[60,1,128]{2,1,0:T(1,128)S(1)}, u32[]{:S(2)}, u32[]{:S(2)}) collective-permute-start(f32[60,1,128]{2,1,0:T(1,128)S(1)} %get-tuple-element.97), channel_id=1, source_target_pairs={{0,8},{8,16},{16,24},{1,9},{9,17},{17,25},{2,10},{10,18},{18,26},{... | collective-permute-start | bytes 92168 | tf_op jit(solution)/shard_map/ppermute | solution.py:21
  7.1 1.3 collective-permute-start.1
  8.5 9.0 %reduce-window.6 = s32[32,8,128]{2,1,0:T(8,128)S(1)} reduce-window(s32[32,8,128]{2,1,0:T(8,128)S(1)} %fusion.157, s32[]{:T(128)} %constant.61.clone.1), window={size=1x1x128 pad=0_0x0_0x127_0}, to_apply=%region_0.0 | reduce-window | flops 4161536 | bytes 262148 | tf_op jit(solution)/shard_map/reduce-window
  18.1 13.0 %while.13 = (s32[]{:T(128)}, bf16[4,512,256]{2,1,0:T(8,128)(2,1)}, s32[4,512]{1,0:T(4,128)S(1)}, s32[4]{0:T(128)S(1)}, s32[1024]{0:T(1024)S(1)}, /*index=5*/bf16...) while((s32[]{:T(128)}, bf16[4,512,256]{2,1,0:T(8,128)(2,1)}, s32[4,512]{1,0:T(4,128)S(1)}, ...), condition=%wide.region_6.7_spmd, body=%wide.region_3.0_spmd.sunk | while | flops 271712256 | bytes 822897 | solution.py:120
  20.2 1.2 fusion.188
  26.7 1.2 fusion.188
  29.9 1.2 fusion.188
  31.8 7.8 %all-to-all-start.1 = ((s32[32,1,64]{2,1,0:T(1,128)}), s32[32,1,64]{2,1,0:T(1,128)}, u32[]{:S(2)}, u32[]{:S(2)}) async-start(s32[32,1,64]{2,1,0:T(1,128)} %all_to_all.10), calls=%async_computation.1 | async-start | bytes 32768 | tf_op jit(solution)/shard_map/all_to_all | solution.py:131
  39.6 1.4 fusion.173
  41.9 2.1 %fusion.166 = (f32[60,66,1]{2,1,0:T(8,128)}, f32[60,66,1]{2,1,0:T(8,128)S(1)}) fusion(f32[60,66,128]{2,1,0:T(8,128)S(1)} %pad_maximum_fusion.3), kind=kLoop, calls=%fused_computation.279 | loop fusion | bytes 63360 | tf_op jit(solution)/shard_map/slice | solution.py:19
  44.0 3.0 %copy.113 = f32[60,66,1]{1,2,0:T(1,128)} copy(f32[60,66,1]{2,1,0:T(8,128)} %get-tuple-element.95) | data formatting | bytes 31680 | tf_op jit(solution)/shard_map/slice | solution.py:19
  47.0 3.5 %collective-permute-start.2 = (f32[60,66,1]{1,2,0:T(1,128)}, f32[60,66,1]{1,2,0:T(1,128)}, u32[]{:S(2)}, u32[]{:S(2)}) collective-permute-start(f32[60,66,1]{1,2,0:T(1,128)} %copy.113), channel_id=1, source_target_pairs={{0,1},{1,2},{2,3},{3,4},{4,5},{5,6},{6,7},{8,9},{9,10},{10,11},{11... | collective-permute-start | bytes 47528 | tf_op jit(solution)/shard_map/ppermute | solution.py:21
  50.5 1.4 copy.115
  51.9 2.0 %collective-permute-start.3 = (f32[60,66,1]{1,2,0:T(1,128)}, f32[60,66,1]{1,2,0:T(1,128)}, u32[]{:S(2)}, u32[]{:S(2)}) collective-permute-start(f32[60,66,1]{1,2,0:T(1,128)} %copy.115), channel_id=1, source_target_pairs={{1,0},{2,1},{3,2},{4,3},{5,4},{6,5},{7,6},{9,8},{10,9},{11,10},{12... | collective-permute-start | bytes 47528 | tf_op jit(solution)/shard_map/ppermute | solution.py:22
  53.9 1.3 slice_bitcast_fusion.11
  55.5 1.2 copy.111
  56.7 6.0 %all-to-all-start = ((bf16[32,64,2,128]{3,1,2,0:T(8,128)(2,1)}), bf16[32,64,2,128]{3,1,2,0:T(8,128)(2,1)}, u32[]{:S(2)}, u32[]{:S(2)}) async-start(bf16[32,64,2,128]{3,1,2,0:T(8,128)(2,1)} %copy.111), calls=%async_computation | async-start | bytes 2097152 | tf_op jit(solution)/shard_map/all_to_all | solution.py:124
  63.3 1.4 reduce.5
  65.3 1.6 copy.114
  67.0 2.9 %copy.116 = f32[60,66,1]{2,1,0:T(8,128)} copy(f32[60,66,1]{1,2,0:T(1,128)} %collective-permute-done.3) | data formatting | bytes 31680 | tf_op jit(solution)/shard_map/ppermute | solution.py:22
  69.9 2.2 %fusion.50 = f32[20,66,128]{2,1,0:T(8,128)S(1)} fusion(f32[60,66,1]{2,1,0:T(8,128)S(1)} %copy.114, f32[60,1,128]{2,1,0:T(1,128)} %copy-done.47, f32[60,1,128]{2,1,0:T(1,128)S(1)} %collective-permute-done, f32[20,64,128]{2,1,0:T(8,128)} %param.13, f32[40,64,128]{2,1,0:T(8,128)S(1)} %bitcast.125, f32[60,66,1]{2,1,0:T(8,128)} %copy.116, f32[60,66,128]{2,1,0:T(8,128)} %copy-done.4), kind=kLoop, calls=%fused_computation.98 | loop fusion | flops 2027520 | bytes 3410880 | tf_op jit(solution)/shard_map/mul | solution.py:70
  72.2 1.9 %fusion.48 = f32[20,66,128]{2,1,0:T(8,128)S(1)} fusion(f32[60,66,1]{2,1,0:T(8,128)S(1)} %copy.114, f32[60,1,128]{2,1,0:T(1,128)S(1)} %copy-done.48, f32[60,1,128]{2,1,0:T(1,128)S(1)} %collective-permute-done, f32[20,64,128]{2,1,0:T(8,128)S(1)} %copy-done.2, f32[40,64,128]{2,1,0:T(8,128)S(1)} %bitcast.126, f32[60,66,1]{2,1,0:T(8,128)S(1)} %copy-done, ...), kind=kLoop, calls=%fused_computation.88 | loop fusion | flops 1858560 | bytes 3410880 | tf_op jit(solution)/shard_map/mul | solution.py:70
  74.0 4.3 %pad_maximum_fusion = f32[60,66,130]{2,1,0:T(8,128)S(1)} fusion(f32[60,66,1]{2,1,0:T(8,128)S(1)} %copy-done, f32[60,1,128]{2,1,0:T(1,128)S(1)} %copy-done.48, f32[20,64,128]{2,1,0:T(8,128)S(1)} %copy-done.2, f32[40,64,128]{2,1,0:T(8,128)S(1)} %bitcast.127, f32[60,1,128]{2,1,0:T(1,128)S(1)} %collective-permute-done, f32[60,66,1]{2,1,0:T(8,128)S(1)} %copy.114), kind=kLoop, calls=%fused_computation.12 | loop fusion | flops 2574000 | bytes 4118400 | tf_op jit(solution)/shard_map/concatenate | solution.py:23
  79.0 1.5 copy-done.3
  81.2 4.5 %fusion.53 = (f32[1,20,64,128]{3,2,1,0:T(8,128)}, f32[20,64,128]{2,1,0:T(8,128)S(1)}, f32[20,64,128]{2,1,0:T(8,128)S(1)}, f32[20,64,128]{2,1,0:T(8,128)S(1)}, f32[20,64,128]{2,1,0:T(8,128)S(1)}) fusion(f32[1,64,128]{2,1,0:T(8,128)S(1)} %bitcast.145, f32[20,64,130]{2,1,0:T(8,128)S(1)} %get-tuple-element.92, f32[20,66,128]{2,1,0:T(8,128)S(1)} %fusion.50, ...), kind=kLoop, calls=%fused_computation.101 | loop fusion | flops 9666560 | bytes 10513344 | tf_op jit(solution)/shard_map/stack | solution.py:79
  85.7 1.4 add_bitcast_fusion.1
  87.9 3.0 %fusion.56 = f32[1,20,64,128]{3,2,1,0:T(8,128)} fusion(f32[1,64,128]{2,1,0:T(8,128)S(1)} %bitcast.147, f32[20,64,130]{2,1,0:T(8,128)S(1)} %get-tuple-element.91, f32[20,66,128]{2,1,0:T(8,128)S(1)} %fusion.48, f32[20,64,128]{2,1,0:T(8,128)S(1)} %get-tuple-element.81, f32[60,66,1]{2,1,0:T(8,128)S(1)} %copy-done, f32[60,1,128]{2,1,0:T(1,128)S(1)} %copy-done.48, ...), kind=kLoop, calls=%fused_computation.104 | loop fusion | flops 6389760 | bytes 10513344 | tf_op jit(solution)/shard_map/stack | solution.py:79
  90.9 1.4 copy.112
  92.9 1.7 fusion.29
  94.7 3.3 %collective-permute-start.4 = (f32[40,1,128]{2,1,0:T(1,128)S(1)}, f32[40,1,128]{2,1,0:T(1,128)S(1)}, u32[]{:S(2)}, u32[]{:S(2)}) collective-permute-start(f32[40,1,128]{2,1,0:T(1,128)S(1)} %get-tuple-element.113), channel_id=1, source_target_pairs={{0,8},{8,16},{16,24},{1,9},{9,17},{17,25},{2,10},{10,18},{18,26},{... | collective-permute-start | bytes 61448 | tf_op jit(solution)/shard_map/ppermute | solution.py:21
  98.0 1.3 collective-permute-start.5
  99.3 1.2 fusion.171
  100.5 2.0 %collective-permute-done.5 = f32[40,1,128]{2,1,0:T(1,128)S(1)} collective-permute-done((f32[40,1,128]{2,1,0:T(1,128)S(1)}, f32[40,1,128]{2,1,0:T(1,128)S(1)}, u32[]{:S(2)}, u32[]{:S(2)}) %collective-permute-start.5) | collective-permute-done | bytes 20512 | tf_op jit(solution)/shard_map/ppermute | solution.py:22
  102.7 2.1 %fusion.168 = (f32[40,66,1]{2,1,0:T(8,128)}, f32[40,66,1]{2,1,0:T(8,128)}) fusion(f32[40,66,128]{2,1,0:T(8,128)S(1)} %pad_maximum_fusion.4), kind=kLoop, calls=%fused_computation.281 | loop fusion | bytes 42240 | tf_op jit(solution)/shard_map/slice | solution.py:19
  104.8 1.9 %copy.121 = f32[40,66,1]{1,0,2:T(8,128)S(1)} copy(f32[40,66,1]{2,1,0:T(8,128)} %get-tuple-element.101) | data formatting | bytes 21120 | tf_op jit(solution)/shard_map/slice | solution.py:19
  106.7 4.8 %collective-permute-start.6 = (f32[40,66,1]{1,0,2:T(8,128)S(1)}, f32[40,66,1]{1,0,2:T(8,128)S(1)}, u32[]{:S(2)}, u32[]{:S(2)}) collective-permute-start(f32[40,66,1]{1,0,2:T(8,128)S(1)} %copy.121), channel_id=1, source_target_pairs={{0,1},{1,2},{2,3},{3,4},{4,5},{5,6},{6,7},{8,9},{9,10},{10,11},{11... | collective-permute-start | bytes 31688 | tf_op jit(solution)/shard_map/ppermute | solution.py:21
  111.5 1.9 %copy.123 = f32[40,66,1]{1,0,2:T(8,128)S(1)} copy(f32[40,66,1]{2,1,0:T(8,128)} %get-tuple-element.102) | data formatting | bytes 21120 | tf_op jit(solution)/shard_map/slice | solution.py:20
  113.4 2.2 %collective-permute-start.7 = (f32[40,66,1]{1,0,2:T(8,128)S(1)}, f32[40,66,1]{1,0,2:T(8,128)S(1)}, u32[]{:S(2)}, u32[]{:S(2)}) collective-permute-start(f32[40,66,1]{1,0,2:T(8,128)S(1)} %copy.123), channel_id=1, source_target_pairs={{1,0},{2,1},{3,2},{4,3},{5,4},{6,5},{7,6},{9,8},{10,9},{11,10},{12... | collective-permute-start | bytes 31688 | tf_op jit(solution)/shard_map/ppermute | solution.py:22
  116.7 1.7 copy.122
  118.5 1.8 %copy.124 = f32[40,66,1]{2,1,0:T(8,128)} copy(f32[40,66,1]{1,0,2:T(8,128)S(1)} %collective-permute-done.7) | data formatting | bytes 21120 | tf_op jit(solution)/shard_map/ppermute | solution.py:22
  120.2 3.2 %pad_maximum_fusion.1 = f32[40,66,130]{2,1,0:T(8,128)S(1)} fusion(f32[40,66,1]{2,1,0:T(8,128)} %copy.124, f32[40,1,128]{2,1,0:T(1,128)S(1)} %collective-permute-done.5, f32[40,64,128]{2,1,0:T(8,128)S(1)} %bitcast.133, f32[40,1,128]{2,1,0:T(1,128)S(1)} %collective-permute-done.4, f32[40,66,1]{2,1,0:T(8,128)} %copy.122), kind=kLoop, calls=%fused_computation.13 | loop fusion | flops 1372800 | bytes 2745600 | tf_op jit(solution)/shard_map/concatenate | solution.py:23
  123.5 2.1 %fusion.21 = (f32[20,64,130]{2,1,0:T(8,128)S(1)}, f32[20,64,130]{2,1,0:T(8,128)S(1)}) fusion(f32[40,66,130]{2,1,0:T(8,128)S(1)} %pad_maximum_fusion.1, f32[60,66,130]{2,1,0:T(8,128)} %copy-done.3), kind=kLoop, calls=%fused_computation.36 | loop fusion | flops 1164800 | bytes 4659200 | tf_op jit(solution)/shard_map/mul | solution.py:72
  125.7 2.7 %fusion.45 = (f32[20,66,128]{2,1,0:T(8,128)S(1)}, f32[20,66,128]{2,1,0:T(8,128)S(1)}) fusion(f32[40,66,1]{2,1,0:T(8,128)S(1)} %copy-done.9, f32[40,1,128]{2,1,0:T(1,128)S(1)} %collective-permute-done.5, f32[40,64,128]{2,1,0:T(8,128)S(1)} %bitcast.134, f32[40,1,128]{2,1,0:T(1,128)S(1)} %collective-permute-done.4, f32[40,66,1]{2,1,0:T(8,128)S(1)} %copy-done.10, ...), kind=kLoop, calls=%fused_computation.84 | loop fusion | flops 3210240 | bytes 3400320 | tf_op jit(solution)/shard_map/mul | solution.py:70
  128.5 1.3 fusion.59
  129.9 1.3 fusion.62
  131.2 1.4 fusion.32
  133.7 1.2 fusion.169
  134.9 4.0 %collective-permute-start.8 = (f32[40,1,128]{2,1,0:T(1,128)S(1)}, f32[40,1,128]{2,1,0:T(1,128)S(1)}, u32[]{:S(2)}, u32[]{:S(2)}) collective-permute-start(f32[40,1,128]{2,1,0:T(1,128)S(1)} %get-tuple-element.105), channel_id=1, source_target_pairs={{0,8},{8,16},{16,24},{1,9},{9,17},{17,25},{2,10},{10,18},{18,26},{... | collective-permute-start | bytes 61448 | tf_op jit(solution)/shard_map/ppermute | solution.py:21
  138.9 1.3 collective-permute-start.9
  141.1 2.3 %collective-permute-done.9 = f32[40,1,128]{2,1,0:T(1,128)S(1)} collective-permute-done((f32[40,1,128]{2,1,0:T(1,128)S(1)}, f32[40,1,128]{2,1,0:T(1,128)S(1)}, u32[]{:S(2)}, u32[]{:S(2)}) %collective-permute-start.9) | collective-permute-done | bytes 20512 | tf_op jit(solution)/shard_map/ppermute | solution.py:22
  143.6 2.1 %fusion.167 = (f32[40,66,1]{2,1,0:T(8,128)}, f32[40,66,1]{2,1,0:T(8,128)}) fusion(f32[40,66,128]{2,1,0:T(8,128)S(1)} %pad_maximum_fusion.5), kind=kLoop, calls=%fused_computation.280 | loop fusion | bytes 42240 | tf_op jit(solution)/shard_map/slice | solution.py:19
  145.7 1.9 %copy.131 = f32[40,66,1]{1,0,2:T(8,128)S(1)} copy(f32[40,66,1]{2,1,0:T(8,128)} %get-tuple-element.99) | data formatting | bytes 21120 | tf_op jit(solution)/shard_map/slice | solution.py:19
  147.6 5.0 %collective-permute-start.10 = (f32[40,66,1]{1,0,2:T(8,128)S(1)}, f32[40,66,1]{1,0,2:T(8,128)S(1)}, u32[]{:S(2)}, u32[]{:S(2)}) collective-permute-start(f32[40,66,1]{1,0,2:T(8,128)S(1)} %copy.131), channel_id=1, source_target_pairs={{0,1},{1,2},{2,3},{3,4},{4,5},{5,6},{6,7},{8,9},{9,10},{10,11},{11... | collective-permute-start | bytes 31688 | tf_op jit(solution)/shard_map/ppermute | solution.py:21
  152.6 1.9 %copy.133 = f32[40,66,1]{1,0,2:T(8,128)S(1)} copy(f32[40,66,1]{2,1,0:T(8,128)} %get-tuple-element.100) | data formatting | bytes 21120 | tf_op jit(solution)/shard_map/slice | solution.py:20
  154.5 2.2 %collective-permute-start.11 = (f32[40,66,1]{1,0,2:T(8,128)S(1)}, f32[40,66,1]{1,0,2:T(8,128)S(1)}, u32[]{:S(2)}, u32[]{:S(2)}) collective-permute-start(f32[40,66,1]{1,0,2:T(8,128)S(1)} %copy.133), channel_id=1, source_target_pairs={{1,0},{2,1},{3,2},{4,3},{5,4},{6,5},{7,6},{9,8},{10,9},{11,10},{12... | collective-permute-start | bytes 31688 | tf_op jit(solution)/shard_map/ppermute | solution.py:22
  156.7 2.0 %slice_bitcast_fusion.6 = f32[19,64,128]{2,1,0:T(8,128)} fusion(f32[2,20,64,128]{3,2,0,1:T(8,128)} %copy-done.23), kind=kLoop, calls=%fused_computation.250 | loop fusion | bytes 1245184 | tf_op jit(solution)/shard_map/slice | solution.py:57
  158.7 1.7 copy.132
  160.4 1.8 %copy.134 = f32[40,66,1]{2,1,0:T(8,128)} copy(f32[40,66,1]{1,0,2:T(8,128)S(1)} %collective-permute-done.11) | data formatting | bytes 21120 | tf_op jit(solution)/shard_map/ppermute | solution.py:22
  162.1 3.2 %pad_maximum_fusion.2 = f32[40,66,130]{2,1,0:T(8,128)S(1)} fusion(f32[40,66,1]{2,1,0:T(8,128)} %copy.134, f32[40,1,128]{2,1,0:T(1,128)S(1)} %collective-permute-done.9, f32[40,64,128]{2,1,0:T(8,128)S(1)} %bitcast.140, f32[40,1,128]{2,1,0:T(1,128)S(1)} %collective-permute-done.8, f32[40,66,1]{2,1,0:T(8,128)} %copy.132), kind=kLoop, calls=%fused_computation.14 | loop fusion | flops 1372800 | bytes 2745600 | tf_op jit(solution)/shard_map/concatenate | solution.py:23
  165.4 2.1 %fusion.17 = (f32[20,64,130]{2,1,0:T(8,128)S(1)}, f32[20,64,130]{2,1,0:T(8,128)S(1)}) fusion(f32[40,66,130]{2,1,0:T(8,128)S(1)} %pad_maximum_fusion.2, f32[60,66,130]{2,1,0:T(8,128)} %copy-done.3), kind=kLoop, calls=%fused_computation.30 | loop fusion | flops 1164800 | bytes 4659200 | tf_op jit(solution)/shard_map/mul | solution.py:72
  167.6 2.7 %fusion.40 = (f32[20,66,128]{2,1,0:T(8,128)S(1)}, f32[20,66,128]{2,1,0:T(8,128)S(1)}) fusion(f32[40,66,1]{2,1,0:T(8,128)S(1)} %copy-done.7, f32[40,1,128]{2,1,0:T(1,128)S(1)} %collective-permute-done.9, f32[40,64,128]{2,1,0:T(8,128)S(1)} %bitcast.141, f32[40,1,128]{2,1,0:T(1,128)S(1)} %collective-permute-done.8, f32[40,66,1]{2,1,0:T(8,128)S(1)} %copy-done.8, ...), kind=kLoop, calls=%fused_computation.72 | loop fusion | flops 3210240 | bytes 3400320 | tf_op jit(solution)/shard_map/mul | solution.py:70
  170.4 1.3 fusion.65
  171.7 1.2 fusion.68
  (181 shorter events, 22.8 us)
Async XLA Ops:
  1.4 1.5 copy-start.43
  1.4 1.6 copy-start.1
  2.9 5.5 %copy-start.54 = (s32[1024,1]{0,1:T(1,128)S(1)}, s32[1024,1]{0,1:T(1,128)}, u32[]{:S(2)}) copy-start(s32[1024,1]{0,1:T(1,128)} %param.18) | copy-start | bytes 12292
  3.0 15.0 %copy-start.50 = (bf16[1024,2,128]{2,1,0:T(2,128)(2,1)S(1)}, bf16[1024,2,128]{2,1,0:T(2,128)(2,1)}, u32[]{:S(2)}) copy-start(bf16[1024,2,128]{2,1,0:T(2,128)(2,1)} %param.17) | copy-start | bytes 1572868
  3.0 15.1 %copy-start.52 = (s32[1024]{0:T(1024)S(1)}, s32[1024]{0:T(1024)}, u32[]{:S(2)}) copy-start(s32[1024]{0:T(1024)} %param.19) | copy-start | bytes 12292
  3.0 37.9 %collective-permute-start = (f32[60,1,128]{2,1,0:T(1,128)S(1)}, f32[60,1,128]{2,1,0:T(1,128)S(1)}, u32[]{:S(2)}, u32[]{:S(2)}) collective-permute-start(f32[60,1,128]{2,1,0:T(1,128)S(1)} %get-tuple-element.97), channel_id=1, source_target_pairs={{0,8},{8,16},{16,24},{1,9},{9,17},{17,25},{2,10},{10,18},{18,26},{... | collective-permute-start | bytes 92168 | tf_op jit(solution)/shard_map/ppermute | solution.py:21
  7.1 33.8 %collective-permute-start.1 = (f32[60,1,128]{2,1,0:T(1,128)S(1)}, f32[60,1,128]{2,1,0:T(1,128)S(1)}, u32[]{:S(2)}, u32[]{:S(2)}) collective-permute-start(f32[60,1,128]{2,1,0:T(1,128)S(1)} %get-tuple-element.98), channel_id=1, source_target_pairs={{8,0},{16,8},{24,16},{9,1},{17,9},{25,17},{10,2},{18,10},{26,18},{... | collective-permute-start | bytes 92168 | tf_op jit(solution)/shard_map/ppermute | solution.py:22
  31.8 24.9 %all-to-all-start.1 = ((s32[32,1,64]{2,1,0:T(1,128)}), s32[32,1,64]{2,1,0:T(1,128)}, u32[]{:S(2)}, u32[]{:S(2)}) async-start(s32[32,1,64]{2,1,0:T(1,128)} %all_to_all.10), calls=%async_computation.1 | async-start | bytes 32768 | tf_op jit(solution)/shard_map/all_to_all | solution.py:131
  40.9 33.1 %copy-start.45 = (f32[60,1,128]{2,1,0:T(1,128)}, f32[60,1,128]{2,1,0:T(1,128)S(1)}, u32[]{:S(2)}) copy-start(f32[60,1,128]{2,1,0:T(1,128)S(1)} %collective-permute-done) | copy-start | bytes 92164
  41.9 2.1 %copy-start.4 = (f32[60,66,128]{2,1,0:T(8,128)}, f32[60,66,128]{2,1,0:T(8,128)S(1)}, u32[]{:S(2)}) copy-start(f32[60,66,128]{2,1,0:T(8,128)S(1)} %pad_maximum_fusion.3) | copy-start | bytes 6082564
  47.0 18.4 %collective-permute-start.2 = (f32[60,66,1]{1,2,0:T(1,128)}, f32[60,66,1]{1,2,0:T(1,128)}, u32[]{:S(2)}, u32[]{:S(2)}) collective-permute-start(f32[60,66,1]{1,2,0:T(1,128)} %copy.113), channel_id=1, source_target_pairs={{0,1},{1,2},{2,3},{3,4},{4,5},{5,6},{6,7},{8,9},{9,10},{10,11},{11... | collective-permute-start | bytes 47528 | tf_op jit(solution)/shard_map/ppermute | solution.py:21
  51.9 3.3 %copy-start.49 = (bf16[4,512,256]{2,1,0:T(8,128)(2,1)S(1)}, bf16[4,512,256]{2,1,0:T(8,128)(2,1)}, u32[]{:S(2)}) copy-start(bf16[4,512,256]{2,1,0:T(8,128)(2,1)} %get-tuple-element.52) | copy-start | bytes 3145732
  51.9 15.1 %collective-permute-start.3 = (f32[60,66,1]{1,2,0:T(1,128)}, f32[60,66,1]{1,2,0:T(1,128)}, u32[]{:S(2)}, u32[]{:S(2)}) collective-permute-start(f32[60,66,1]{1,2,0:T(1,128)} %copy.115), channel_id=1, source_target_pairs={{1,0},{2,1},{3,2},{4,3},{5,4},{6,5},{7,6},{9,8},{10,9},{11,10},{12... | collective-permute-start | bytes 47528 | tf_op jit(solution)/shard_map/ppermute | solution.py:22
  56.7 34.2 %all-to-all-start = ((bf16[32,64,2,128]{3,1,2,0:T(8,128)(2,1)}), bf16[32,64,2,128]{3,1,2,0:T(8,128)(2,1)}, u32[]{:S(2)}, u32[]{:S(2)}) async-start(bf16[32,64,2,128]{3,1,2,0:T(8,128)(2,1)} %copy.111), calls=%async_computation | async-start | bytes 2097152 | tf_op jit(solution)/shard_map/all_to_all | solution.py:124
  69.9 2.3 %copy-start = (f32[60,66,1]{2,1,0:T(8,128)S(1)}, f32[60,66,1]{2,1,0:T(8,128)}, u32[]{:S(2)}) copy-start(f32[60,66,1]{2,1,0:T(8,128)} %copy.116) | copy-start | bytes 47524
  69.9 2.3 %copy-start.2 = (f32[20,64,128]{2,1,0:T(8,128)S(1)}, f32[20,64,128]{2,1,0:T(8,128)}, u32[]{:S(2)}) copy-start(f32[20,64,128]{2,1,0:T(8,128)} %param.13) | copy-start | bytes 1966084
  69.9 2.3 %copy-start.48 = (f32[60,1,128]{2,1,0:T(1,128)S(1)}, f32[60,1,128]{2,1,0:T(1,128)}, u32[]{:S(2)}) copy-start(f32[60,1,128]{2,1,0:T(1,128)} %copy-done.47) | copy-start | bytes 92164
  78.3 2.2 %copy-start.3 = (f32[60,66,130]{2,1,0:T(8,128)}, f32[60,66,130]{2,1,0:T(8,128)S(1)}, u32[]{:S(2)}) copy-start(f32[60,66,130]{2,1,0:T(8,128)S(1)} %pad_maximum_fusion) | copy-start | bytes 6177604
  78.3 2.2 %copy-start.5 = (f32[19,64,128]{2,1,0:T(8,128)S(1)}, f32[19,64,128]{2,1,0:T(8,128)}, u32[]{:S(2)}) copy-start(f32[19,64,128]{2,1,0:T(8,128)} %get-tuple-element.119) | copy-start | bytes 1867780
  78.3 2.2 %copy-start.40 = (f32[19,64,128]{2,1,0:T(8,128)S(1)}, f32[19,64,128]{2,1,0:T(8,128)}, u32[]{:S(2)}) copy-start(f32[19,64,128]{2,1,0:T(8,128)} %get-tuple-element.117) | copy-start | bytes 1867780
  78.4 2.8 %copy-start.41 = (f32[19,64,128]{2,1,0:T(8,128)S(1)}, f32[19,64,128]{2,1,0:T(8,128)}, u32[]{:S(2)}) copy-start(f32[19,64,128]{2,1,0:T(8,128)} %get-tuple-element.118) | copy-start | bytes 1867780
  78.4 2.8 %copy-start.42 = (f32[64,128]{1,0:T(8,128)S(1)}, f32[64,128]{1,0:T(8,128)}, u32[]{:S(2)}) copy-start(f32[64,128]{1,0:T(8,128)} %param.14) | copy-start | bytes 98308
  78.4 2.8 %copy-start.46 = (f32[60,1,128]{2,1,0:T(1,128)S(1)}, f32[60,1,128]{2,1,0:T(1,128)}, u32[]{:S(2)}) copy-start(f32[60,1,128]{2,1,0:T(1,128)} %copy-done.45) | copy-start | bytes 92164
  85.7 1.4 copy-start.11
  85.7 1.5 copy-start.14
  85.7 1.7 copy-start.17
  85.7 2.0 %copy-start.20 = (f32[20,64,128]{2,1,0:T(8,128)}, f32[20,64,128]{2,1,0:T(8,128)S(1)}, u32[]{:S(2)}) copy-start(f32[20,64,128]{2,1,0:T(8,128)S(1)} %get-tuple-element.82) | copy-start | bytes 1966084
  85.7 2.0 %copy-start.33 = (f32[19,64,128]{2,1,0:T(8,128)S(1)}, f32[19,64,128]{2,1,0:T(8,128)}, u32[]{:S(2)}) copy-start(f32[19,64,128]{2,1,0:T(8,128)} %get-tuple-element.115) | copy-start | bytes 1867780
  85.7 2.2 %copy-start.34 = (f32[19,64,128]{2,1,0:T(8,128)S(1)}, f32[19,64,128]{2,1,0:T(8,128)}, u32[]{:S(2)}) copy-start(f32[19,64,128]{2,1,0:T(8,128)} %get-tuple-element.116) | copy-start | bytes 1867780
  90.9 1.5 copy-start.55
  90.9 1.8 %copy-start.24 = (f32[1,20,64,128]{3,2,1,0:T(8,128)S(1)}, f32[1,20,64,128]{3,2,1,0:T(8,128)}, u32[]{:S(2)}) copy-start(f32[1,20,64,128]{3,2,1,0:T(8,128)} %get-tuple-element.93) | copy-start | bytes 1966084
  90.9 1.8 %copy-start.26 = (f32[1,20,64,128]{3,2,1,0:T(8,128)S(1)}, f32[1,20,64,128]{3,2,1,0:T(8,128)}, u32[]{:S(2)}) copy-start(f32[1,20,64,128]{3,2,1,0:T(8,128)} %get-tuple-element.94) | copy-start | bytes 1966084
  90.9 1.8 %copy-start.44 = (f32[64,128]{1,0:T(8,128)S(1)}, f32[64,128]{1,0:T(8,128)}, u32[]{:S(2)}) copy-start(f32[64,128]{1,0:T(8,128)} %copy-done.43) | copy-start | bytes 98308
  90.9 2.0 %copy-start.29 = (f32[2,20,64,128]{3,2,1,0:T(8,128)S(1)}, f32[2,20,64,128]{3,2,1,0:T(8,128)}, u32[]{:S(2)}) copy-start(f32[2,20,64,128]{3,2,1,0:T(8,128)} %param.12) | copy-start | bytes 3932164
  94.7 5.8 %collective-permute-start.4 = (f32[40,1,128]{2,1,0:T(1,128)S(1)}, f32[40,1,128]{2,1,0:T(1,128)S(1)}, u32[]{:S(2)}, u32[]{:S(2)}) collective-permute-start(f32[40,1,128]{2,1,0:T(1,128)S(1)} %get-tuple-element.113), channel_id=1, source_target_pairs={{0,8},{8,16},{16,24},{1,9},{9,17},{17,25},{2,10},{10,18},{18,26},{... | collective-permute-start | bytes 61448 | tf_op jit(solution)/shard_map/ppermute | solution.py:21
  98.0 4.5 %collective-permute-start.5 = (f32[40,1,128]{2,1,0:T(1,128)S(1)}, f32[40,1,128]{2,1,0:T(1,128)S(1)}, u32[]{:S(2)}, u32[]{:S(2)}) collective-permute-start(f32[40,1,128]{2,1,0:T(1,128)S(1)} %get-tuple-element.114), channel_id=1, source_target_pairs={{8,0},{16,8},{24,16},{9,1},{17,9},{25,17},{10,2},{18,10},{26,18},{... | collective-permute-start | bytes 61448 | tf_op jit(solution)/shard_map/ppermute | solution.py:22
  106.7 10.1 %collective-permute-start.6 = (f32[40,66,1]{1,0,2:T(8,128)S(1)}, f32[40,66,1]{1,0,2:T(8,128)S(1)}, u32[]{:S(2)}, u32[]{:S(2)}) collective-permute-start(f32[40,66,1]{1,0,2:T(8,128)S(1)} %copy.121), channel_id=1, source_target_pairs={{0,1},{1,2},{2,3},{3,4},{4,5},{5,6},{6,7},{8,9},{9,10},{10,11},{11... | collective-permute-start | bytes 31688 | tf_op jit(solution)/shard_map/ppermute | solution.py:21
  113.4 5.1 %collective-permute-start.7 = (f32[40,66,1]{1,0,2:T(8,128)S(1)}, f32[40,66,1]{1,0,2:T(8,128)S(1)}, u32[]{:S(2)}, u32[]{:S(2)}) collective-permute-start(f32[40,66,1]{1,0,2:T(8,128)S(1)} %copy.123), channel_id=1, source_target_pairs={{1,0},{2,1},{3,2},{4,3},{5,4},{6,5},{7,6},{9,8},{10,9},{11,10},{12... | collective-permute-start | bytes 31688 | tf_op jit(solution)/shard_map/ppermute | solution.py:22
  123.4 2.1 %copy-start.9 = (f32[40,66,1]{2,1,0:T(8,128)S(1)}, f32[40,66,1]{2,1,0:T(8,128)}, u32[]{:S(2)}) copy-start(f32[40,66,1]{2,1,0:T(8,128)} %copy.122) | copy-start | bytes 31684
  123.5 2.3 %copy-start.10 = (f32[40,66,1]{2,1,0:T(8,128)S(1)}, f32[40,66,1]{2,1,0:T(8,128)}, u32[]{:S(2)}) copy-start(f32[40,66,1]{2,1,0:T(8,128)} %copy.124) | copy-start | bytes 31684
  125.7 2.8 %copy-start.6 = (f32[19,64,128]{2,1,0:T(8,128)S(1)}, f32[19,64,128]{2,1,0:T(8,128)}, u32[]{:S(2)}) copy-start(f32[19,64,128]{2,1,0:T(8,128)} %get-tuple-element.119) | copy-start | bytes 1867780
  125.7 2.8 %copy-start.12 = (f32[20,64,128]{2,1,0:T(8,128)S(1)}, f32[20,64,128]{2,1,0:T(8,128)}, u32[]{:S(2)}) copy-start(f32[20,64,128]{2,1,0:T(8,128)} %copy-done.11) | copy-start | bytes 1966084
  125.7 2.8 %copy-start.15 = (f32[20,64,128]{2,1,0:T(8,128)S(1)}, f32[20,64,128]{2,1,0:T(8,128)}, u32[]{:S(2)}) copy-start(f32[20,64,128]{2,1,0:T(8,128)} %copy-done.14) | copy-start | bytes 1966084
  125.7 2.8 %copy-start.18 = (f32[20,64,128]{2,1,0:T(8,128)S(1)}, f32[20,64,128]{2,1,0:T(8,128)}, u32[]{:S(2)}) copy-start(f32[20,64,128]{2,1,0:T(8,128)} %copy-done.17) | copy-start | bytes 1966084
  125.7 2.8 %copy-start.21 = (f32[20,64,128]{2,1,0:T(8,128)S(1)}, f32[20,64,128]{2,1,0:T(8,128)}, u32[]{:S(2)}) copy-start(f32[20,64,128]{2,1,0:T(8,128)} %copy-done.20) | copy-start | bytes 1966084
  125.7 2.8 %copy-start.35 = (f32[19,64,128]{2,1,0:T(8,128)S(1)}, f32[19,64,128]{2,1,0:T(8,128)}, u32[]{:S(2)}) copy-start(f32[19,64,128]{2,1,0:T(8,128)} %get-tuple-element.109) | copy-start | bytes 1867780
  125.7 2.8 %copy-start.36 = (f32[19,64,128]{2,1,0:T(8,128)S(1)}, f32[19,64,128]{2,1,0:T(8,128)}, u32[]{:S(2)}) copy-start(f32[19,64,128]{2,1,0:T(8,128)} %get-tuple-element.110) | copy-start | bytes 1867780
  128.5 1.3 copy-start.38
  128.5 1.3 copy-start.39
  129.9 1.3 copy-start.25
  129.9 1.3 copy-start.27
  134.9 6.2 %collective-permute-start.8 = (f32[40,1,128]{2,1,0:T(1,128)S(1)}, f32[40,1,128]{2,1,0:T(1,128)S(1)}, u32[]{:S(2)}, u32[]{:S(2)}) collective-permute-start(f32[40,1,128]{2,1,0:T(1,128)S(1)} %get-tuple-element.105), channel_id=1, source_target_pairs={{0,8},{8,16},{16,24},{1,9},{9,17},{17,25},{2,10},{10,18},{18,26},{... | collective-permute-start | bytes 61448 | tf_op jit(solution)/shard_map/ppermute | solution.py:21
  138.9 4.5 %collective-permute-start.9 = (f32[40,1,128]{2,1,0:T(1,128)S(1)}, f32[40,1,128]{2,1,0:T(1,128)S(1)}, u32[]{:S(2)}, u32[]{:S(2)}) collective-permute-start(f32[40,1,128]{2,1,0:T(1,128)S(1)} %get-tuple-element.106), channel_id=1, source_target_pairs={{8,0},{16,8},{24,16},{9,1},{17,9},{25,17},{10,2},{18,10},{26,18},{... | collective-permute-start | bytes 61448 | tf_op jit(solution)/shard_map/ppermute | solution.py:22
  147.6 11.1 %collective-permute-start.10 = (f32[40,66,1]{1,0,2:T(8,128)S(1)}, f32[40,66,1]{1,0,2:T(8,128)S(1)}, u32[]{:S(2)}, u32[]{:S(2)}) collective-permute-start(f32[40,66,1]{1,0,2:T(8,128)S(1)} %copy.131), channel_id=1, source_target_pairs={{0,1},{1,2},{2,3},{3,4},{4,5},{5,6},{6,7},{8,9},{9,10},{10,11},{11... | collective-permute-start | bytes 31688 | tf_op jit(solution)/shard_map/ppermute | solution.py:21
  154.5 5.9 %collective-permute-start.11 = (f32[40,66,1]{1,0,2:T(8,128)S(1)}, f32[40,66,1]{1,0,2:T(8,128)S(1)}, u32[]{:S(2)}, u32[]{:S(2)}) collective-permute-start(f32[40,66,1]{1,0,2:T(8,128)S(1)} %copy.133), channel_id=1, source_target_pairs={{1,0},{2,1},{3,2},{4,3},{5,4},{6,5},{7,6},{9,8},{10,9},{11,10},{12... | collective-permute-start | bytes 31688 | tf_op jit(solution)/shard_map/ppermute | solution.py:22
  165.3 2.2 %copy-start.7 = (f32[40,66,1]{2,1,0:T(8,128)S(1)}, f32[40,66,1]{2,1,0:T(8,128)}, u32[]{:S(2)}) copy-start(f32[40,66,1]{2,1,0:T(8,128)} %copy.132) | copy-start | bytes 31684
  165.4 2.3 %copy-start.8 = (f32[40,66,1]{2,1,0:T(8,128)S(1)}, f32[40,66,1]{2,1,0:T(8,128)}, u32[]{:S(2)}) copy-start(f32[40,66,1]{2,1,0:T(8,128)} %copy.134) | copy-start | bytes 31684
  167.6 2.7 %copy-start.13 = (f32[20,64,128]{2,1,0:T(8,128)S(1)}, f32[20,64,128]{2,1,0:T(8,128)}, u32[]{:S(2)}) copy-start(f32[20,64,128]{2,1,0:T(8,128)} %copy-done.11) | copy-start | bytes 1966084
  167.6 2.7 %copy-start.16 = (f32[20,64,128]{2,1,0:T(8,128)S(1)}, f32[20,64,128]{2,1,0:T(8,128)}, u32[]{:S(2)}) copy-start(f32[20,64,128]{2,1,0:T(8,128)} %copy-done.14) | copy-start | bytes 1966084
  167.6 2.8 %copy-start.19 = (f32[20,64,128]{2,1,0:T(8,128)S(1)}, f32[20,64,128]{2,1,0:T(8,128)}, u32[]{:S(2)}) copy-start(f32[20,64,128]{2,1,0:T(8,128)} %copy-done.17) | copy-start | bytes 1966084
  167.6 2.8 %copy-start.22 = (f32[20,64,128]{2,1,0:T(8,128)S(1)}, f32[20,64,128]{2,1,0:T(8,128)}, u32[]{:S(2)}) copy-start(f32[20,64,128]{2,1,0:T(8,128)} %copy-done.20) | copy-start | bytes 1966084
  167.6 2.8 %copy-start.31 = (f32[19,64,128]{2,1,0:T(8,128)S(1)}, f32[19,64,128]{2,1,0:T(8,128)}, u32[]{:S(2)}) copy-start(f32[19,64,128]{2,1,0:T(8,128)} %get-tuple-element.103) | copy-start | bytes 1867780
  167.6 2.8 %copy-start.32 = (f32[19,64,128]{2,1,0:T(8,128)S(1)}, f32[19,64,128]{2,1,0:T(8,128)}, u32[]{:S(2)}) copy-start(f32[19,64,128]{2,1,0:T(8,128)} %get-tuple-element.104) | copy-start | bytes 1867780
  171.7 1.3 copy-start.28
  (6 other events, 6.6 us)
where the time goes:
time: 177 us; the launch traced here: 175 us
  other arithmetic  64.6 us (36%)
  local copies, waits for them, and re-layouts  50.8 us (29%)
  starting transfers between devices  48.7 us (28%)
  matrix products  5.1 us (3%)
  waiting for transfers between devices  4.43 us (3%)
    ppermute x6, starting transfers between devices, with_halo(): before = lax.ppermute(last, axis, up)  24.7 us
    slice x8, local copies, waits for them, and re-layouts, with_halo(): last = lax.slice_in_dim(array, length - width, length, axis=dim)  13.1 us
    another operation x6, other arithmetic, operate(): return jnp.stack([first, second])  12.6 us
    concatenate x6, other arithmetic, with_halo(): array = jnp.concatenate([before, array, after], axis=dim)  11.3 us
    ppermute x6, starting transfers between devices, with_halo(): after = lax.ppermute(initial, axis, down)  10.3 us
    mul x4, other arithmetic, mixed(): flux_x = weight_x * padded_eta[:, :, 1:-1] * along_y  9.51 us
    another operation x3, other arithmetic  9.15 us
    all_to_all x1, starting transfers between devices, on_device(): lax.all_to_all(send_rows.reshape(device_count, capacity), ('gx', 'gy'), s...  7.75 us
  transfers between devices with their start and end apart: 14, of which 3 were waited for; matrix products, arithmetic and copies ran while one was open for 40% of the time, Pallas kernels for 0%

commit v1 on v0

v1 whole, which is shorter than its diff:
```python
import functools
import math

import jax
import jax.numpy as jnp
from jax import lax
from jax.experimental import pallas as pl
from jax.experimental.pallas import tpu as pltpu
from jax.sharding import PartitionSpec as P

ITERS = 3
HALO = ITERS
GROUP = 2 * HALO
PAD_UNITS = 4
VERTICAL = 4.0

F32 = jnp.float32
BF16 = jnp.bfloat16


def omega_list(count):
    return [
        1.0 / (1.3 + 1.2 * math.cos((2 * turn_id + 1) * math.pi / (2 * count)))
        for turn_id in range(count)
    ]


def shift_up(array, axis):
    peers = lax.axis_size(axis)
    return lax.ppermute(array, axis, [(i, i + 1) for i in range(peers - 1)])


def shift_down(array, axis):
    peers = lax.axis_size(axis)
    return lax.ppermute(array, axis, [(i + 1, i) for i in range(peers - 1)])


def vmem_specs(count):
    return [pl.BlockSpec(memory_space=pltpu.VMEM) for _ in range(count)]


def rows_before(values):
    return pltpu.roll(values, 1, 0)


def rows_after(values):
    return pltpu.roll(values, values.shape[0] - 1, 0)


def lanes_before(values, step=1):
    return pltpu.roll(values, step, 1)


def lanes_after(values, step=1):
    return pltpu.roll(values, values.shape[1] - step, 1)


def lane_index(shape):
    return lax.broadcasted_iota(jnp.int32, shape, len(shape) - 1)


def edge_kernel(layers, adj_lo, adj_hi, eta_lo, eta_hi, fr_lo, fr_hi, ice_lo, ice_hi, lo, hi):
    for adj, eta, fr, ice, out, at in (
        (adj_lo, eta_lo, fr_lo, ice_lo, lo, 0),
        (adj_hi, eta_hi, fr_hi, ice_hi, hi, 8 - HALO),
    ):
        rows = slice(at, at + HALO)
        covered = ice[rows, :] > 0
        for plane in range(2 * layers):
            values = jnp.where(covered, adj[plane // layers, plane % layers, rows, :], 0.0)
            out[HALO * plane : HALO * (plane + 1), :] = values
        for layer in range(layers):
            values = eta[layer, rows, :]
            first = HALO * (2 * layers + layer)
            out[first : first + HALO, :] = jnp.where(covered, values, -values)
        first = HALO * 3 * layers
        out[first : first + HALO, :] = fr[rows, :]


def edge_rows(adjoint, viscosity, friction, ice_mask):
    _, layers, rows, cols = adjoint.shape
    last = rows // 8 - 1
    length = -(-HALO * (3 * layers + 1) // 8) * 8

    def pair(block, index):
        return [
            pl.BlockSpec(block, functools.partial(index, 0)),
            pl.BlockSpec(block, functools.partial(index, last)),
        ]

    specs = pair((2, layers, 8, cols), lambda r, i: (0, 0, r, 0))
    specs += pair((layers, 8, cols), lambda r, i: (0, r, 0))
    specs += pair((8, cols), lambda r, i: (r, 0))
    specs += pair((8, cols), lambda r, i: (r, 0))
    return pl.pallas_call(
        functools.partial(edge_kernel, layers),
        grid=(1,),
        in_specs=specs,
        out_specs=[pl.BlockSpec((length, cols), lambda i: (0, 0))] * 2,
        out_shape=[jax.ShapeDtypeStruct((length, cols), F32)] * 2,
        name="edge_rows",
    )(adjoint, adjoint, viscosity, viscosity, friction, friction, ice_mask, ice_mask)


def column_kernel(layers, adj, eta, fr, ice, above, below, u_out, v_out, e_out, f_out, packed):
    rows, cols = fr.shape
    circle = rows + 8
    lane_layer = lane_index((circle, cols)) // GROUP
    covered = ice[...] > 0
    gap = jnp.zeros((8 - 2 * HALO, cols), F32)

    def extend(out, values, plane):
        first = HALO * plane
        out[:rows, :] = values
        out[rows : rows + HALO, :] = below[first : first + HALO, :]
        out[rows + HALO : circle - HALO, :] = gap
        out[circle - HALO : circle, :] = above[first : first + HALO, :]

    def gather(total, values, layer):
        return jnp.where(
            lane_layer == layer, pltpu.roll(values, (HALO + GROUP * layer) % cols, 1), total
        )

    totals = [jnp.zeros((circle, cols), F32)] * 3
    for layer in range(layers):
        extend(u_out.at[layer], jnp.where(covered, adj[0, layer], 0.0), layer)
        extend(v_out.at[layer], jnp.where(covered, adj[1, layer], 0.0), layers + layer)
        values = eta[layer]
        extend(e_out.at[layer], jnp.where(covered, values, -values), 2 * layers + layer)
        for field, out in enumerate((u_out, v_out, e_out)):
            totals[field] = gather(totals[field], out[layer], layer)
    extend(f_out, fr[...], 3 * layers)
    totals[2] = gather(totals[2], f_out[...], layers)
    for field in range(3):
        packed[field] = totals[field]


def edge_columns(adjoint, viscosity, friction, ice_mask, above, below):
    _, layers, rows, cols = adjoint.shape
    circle = rows + 8
    field = jax.ShapeDtypeStruct((layers, circle, cols), F32)
    return pl.pallas_call(
        functools.partial(column_kernel, layers),
        in_specs=vmem_specs(6),
        out_specs=vmem_specs(5),
        out_shape=[
            field,
            field,
            field,
            jax.ShapeDtypeStruct((circle, cols), F32),
            jax.ShapeDtypeStruct((3, circle, cols), F32),
        ],
        name="edge_columns",
    )(adjoint, viscosity, friction, ice_mask, above, below)


def strip_step(eta, scale, fields, omega, sources=None):
    parts = []
    for f in fields:
        p = eta * f
        y_low, y_high = lanes_before(f), lanes_after(f)
        x_low, x_high = rows_before(f), rows_after(f)
        parts.append(
            dict(
                p=p,
                sum_x=x_low + x_high,
                sum_y=y_low + y_high,
                sum_z=lanes_before(f, GROUP) + lanes_after(f, GROUP),
                p_z=lanes_before(p, GROUP) + lanes_after(p, GROUP),
                g=eta * (y_high - y_low),
                h=eta * (x_high - x_low),
            )
        )
    news, lows, highs = [], [], []
    for c in range(2):
        mine, other = parts[c], parts[1 - c]
        wg, wh = (0.25, 0.5) if c == 0 else (0.5, 0.25)
        cross_x, cross_y = wg * other["g"], wh * other["h"]
        low, high = mine["p"] - cross_y, mine["p"] + cross_y
        lows.append(low)
        highs.append(high)
        if omega is None:
            continue
        along_x = rows_after(mine["p"] + cross_x) + rows_before(mine["p"] - cross_x)
        along_y = lanes_after(high) + lanes_before(low)
        if c == 0:
            near = mine["sum_x"] + mine["sum_z"] + 0.25 * mine["sum_y"]
            rest = along_x + mine["p_z"] + 0.25 * along_y
        else:
            near = mine["sum_y"] + mine["sum_z"] + 0.25 * mine["sum_x"]
            rest = along_y + mine["p_z"] + 0.25 * along_x
        total = eta * near + rest
        if sources is not None:
            total = total + 0.5 * sources[c]
        news.append((1.0 - omega) * fields[c] + omega * (scale[c] * total))
    return news, lows, highs


def joined(left, right, column):
    return jnp.where(column == HALO - 1, left, right)


def plane_step(k, lane, eta, fields, products, scale, edges, sums, omega, source=None):
    shift = GROUP * k + HALO
    shape = lane.shape
    back = shape[1] - shift
    first, last = lane == 0, lane == shape[1] - 1
    e = eta[k + 1]
    parts = []
    for c in range(2):
        f = fields[c, k + 1]
        edge = pltpu.roll(edges[c], back, 1)
        y_low = lanes_before(jnp.where(last, edge, f))
        y_high = lanes_after(jnp.where(first, edge, f))
        x_low, x_high = rows_before(f), rows_after(f)
        parts.append(
            dict(
                f=f,
                p=products[c, k + 1],
                sum_x=x_low + x_high,
                sum_y=y_low + y_high,
                g=e * (y_high - y_low),
                h=e * (x_high - x_low),
            )
        )
    news = []
    for c in range(2):
        mine, other = parts[c], parts[1 - c]
        wg, wh = (0.25, 0.5) if c == 0 else (0.5, 0.25)
        cross_x, cross_y = wg * other["g"], wh * other["h"]
        p = mine["p"]
        edge = pltpu.roll(sums[c], back, 1)
        along_x = rows_after(p + cross_x) + rows_before(p - cross_x)
        along_y = lanes_after(jnp.where(first, edge, p + cross_y))
        along_y = along_y + lanes_before(jnp.where(last, edge, p - cross_y))
        sum_z = fields[c, k] + fields[c, k + 2]
        p_z = products[c, k] + products[c, k + 2]
        if c == 0:
            near = mine["sum_x"] + sum_z + 0.25 * mine["sum_y"]
            rest = along_x + p_z + 0.25 * along_y
        else:
            near = mine["sum_y"] + sum_z + 0.25 * mine["sum_x"]
            rest = along_y + p_z + 0.25 * along_x
        total = e * near + rest
        if source is not None:
            total = total + source[c]
        news.append((1.0 - omega) * mine["f"] + omega * (scale[c, k] * total))
    return news


def inverse_pair(e, e_x, e_y, e_z, ends, basal, covered):
    vertical = (VERTICAL / 2) * (e_z + ends * e) + basal
    both_x, both_y = e_x + 2.0 * e, e_y + 2.0 * e
    out = []
    for wx, wy in ((2.0, 0.5), (0.5, 2.0)):
        diagonal = wx * both_x + wy * both_y + vertical
        safe = jnp.where(covered, diagonal, 1.0)
        out.append(jnp.where(covered, 2.0 / safe, 0.0))
    return out


def sweep_kernel(
    layers,
    u_in, v_in, e_in, f_in, packed, packed_left, packed_right, basal_velocity,
    out, gradient, scale_out, eta_out, strip_out,
    fields, products, eta, scale, edges, sums,
):
    circle, cols = f_in.shape
    rows = out.shape[2]
    lane = lane_index((circle, cols))
    column = lane % GROUP
    omegas = omega_list(ITERS)
    zero = jnp.zeros((circle, cols), F32)

    strips = []
    for side in range(2):
        values = []
        for field in range(3):
            own = packed[field]
            if side == 0:
                values.append(jnp.where(column < HALO, packed_left[field], own))
            else:
                values.append(jnp.where(column < HALO, own, packed_right[field]))
        signed = values[2]
        inside = lane < GROUP * layers
        bottom = inside & (lane >= GROUP * (layers - 1))
        covered = inside & (signed > 0.0)
        e = jnp.where(inside, jnp.abs(signed), 0.0)
        basal = jnp.where(bottom, lanes_after(signed, GROUP), 0.0)
        ends = jnp.where(bottom | (lane < GROUP), 1.0, 2.0)
        pair = inverse_pair(
            e,
            rows_before(e) + rows_after(e),
            lanes_before(e) + lanes_after(e),
            lanes_before(e, GROUP) + lanes_after(e, GROUP),
            ends,
            basal,
            covered,
        )
        strip_out[side, 0] = e
        strip_out[side, 1] = pair[0]
        strip_out[side, 2] = pair[1]
        strips.append((e, pair, values[:2]))
    eta_edge = joined(strips[0][0], strips[1][0], column)
    states = [strips[0][2], strips[1][2]]
    for turn, omega in enumerate(omegas):
        step = omega if turn < ITERS - 1 else None
        left, lows, _ = strip_step(strips[0][0], strips[0][1], states[0], step)
        right, _, highs = strip_step(strips[1][0], strips[1][1], states[1], step)
        for c in range(2):
            edges[turn, c] = joined(states[0][c], states[1][c], column)
            sums[turn, c] = joined(lows[c], highs[c], column)
        states = [left, right]

    for stack in (eta, fields.at[0, 0], fields.at[0, 1], fields.at[1, 0], fields.at[1, 1]):
        stack[0] = zero
        stack[layers + 1] = zero
    for half in range(2):
        for c in range(2):
            products[half, c, 0] = zero
            products[half, c, layers + 1] = zero

    def load(k, carry):
        e = jnp.abs(e_in[k])
        eta[k + 1] = e
        for c, values in enumerate((u_in, v_in)):
            f = values[k]
            fields[0, c, k + 1] = f
            products[0, c, k + 1] = e * f
        return carry

    lax.fori_loop(0, layers, load, 0)

    def weigh(k, carry):
        e = eta[k + 1]
        edge = pltpu.roll(eta_edge, cols - (GROUP * k + HALO), 1)
        e_y = lanes_before(jnp.where(lane == cols - 1, edge, e))
        e_y = e_y + lanes_after(jnp.where(lane == 0, edge, e))
        is_end = (k == 0) | (k == layers - 1)
        ends = jnp.where(is_end, 1.0, 2.0)
        basal = jnp.where(k == layers - 1, 1.0, 0.0) * f_in[...]
        pair = inverse_pair(
            e,
            rows_before(e) + rows_after(e),
            e_y,
            eta[k] + eta[k + 2],
            ends,
            basal,
            e_in[k] > 0.0,
        )
        scale[0, k] = pair[0]
        scale[1, k] = pair[1]
        return carry

    lax.fori_loop(0, layers, weigh, 0)

    for turn, omega in enumerate(omegas):
        half, final = turn % 2, turn == ITERS - 1
        near = (edges.at[turn], sums.at[turn])

        def sweep(k, carry, half=half, final=final, near=near, omega=omega):
            pair = plane_step(
                k, lane, eta, fields.at[half], products.at[half], scale,
                (near[0][0], near[0][1]), (near[1][0], near[1][1]), omega,
            )
            for c in range(2):
                if final:
                    out[c, k] = pair[c][:rows]
                else:
                    fields[1 - half, c, k + 1] = pair[c]
                    products[1 - half, c, k + 1] = eta[k + 1] * pair[c]
            return carry

        lax.fori_loop(0, layers, sweep, 0)

    covered = e_in[layers - 1][:rows] > 0.0
    flow = basal_velocity[0] * out[0, layers - 1] + basal_velocity[1] * out[1, layers - 1]
    gradient[...] = jnp.where(covered, -f_in[...][:rows] * flow, 0.0)
    for k in range(ITERS):
        for c in range(2):
            scale_out[c, k] = scale[c, k]
    for k in range(ITERS + 1):
        eta_out[k] = eta[k + 1]


def free_sweeps(u, v, e, f, packed, left, right, basal_velocity):
    layers, circle, cols = u.shape
    rows = basal_velocity.shape[1]
    plane = (circle, cols)
    stack = (layers + 2,) + plane
    return pl.pallas_call(
        functools.partial(sweep_kernel, layers),
        in_specs=vmem_specs(8),
        out_specs=vmem_specs(5),
        out_shape=[
            jax.ShapeDtypeStruct((2, layers, rows, cols), F32),
            jax.ShapeDtypeStruct((rows, cols), F32),
            jax.ShapeDtypeStruct((2, ITERS) + plane, F32),
            jax.ShapeDtypeStruct((ITERS + 1,) + plane, F32),
            jax.ShapeDtypeStruct((2, 3) + plane, F32),
        ],
        scratch_shapes=[
            pltpu.VMEM((2, 2) + stack, F32),
            pltpu.VMEM((2, 2) + stack, F32),
            pltpu.VMEM(stack, F32),
            pltpu.VMEM((2, layers) + plane, F32),
            pltpu.VMEM((ITERS, 2) + plane, F32),
            pltpu.VMEM((ITERS, 2) + plane, F32),
        ],
        cost_estimate=pl.CostEstimate(
            flops=200_000_000, transcendentals=0, bytes_accessed=8_000_000
        ),
        name="free_sweeps",
    )(u, v, e, f, packed, left, right, basal_velocity)


def pack_kernel(devices, capacity, units, tile, row, misfit, out, slot_vector, slot, sem):
    turns, lanes = tile.shape
    device = lax.broadcasted_iota(jnp.int32, (devices, lanes), 0)
    at_row = lax.broadcasted_iota(jnp.int32, (lanes, lanes), 0)
    at_lane = lax.broadcasted_iota(jnp.int32, (lanes, lanes), 1)
    earlier = jnp.where(at_row < at_lane, 1.0, 0.0).astype(BF16)
    seen = jnp.zeros((devices, 1), F32)
    keys = jnp.zeros((devices, lanes), F32)
    for turn in range(turns):
        target = tile[turn : turn + 1, :]
        onehot = jnp.where(device == target, 1.0, 0.0)
        before = jnp.dot(onehot.astype(BF16), earlier, preferred_element_type=F32) + seen
        rank = jnp.sum(onehot * before, axis=0, keepdims=True).astype(jnp.int32)
        slot_vector[turn : turn + 1, :] = target * units + rank
        seen = seen + jnp.sum(onehot, axis=1, keepdims=True)
        named = onehot * (row[turn : turn + 1, :] + 1).astype(F32)
        place = jnp.where(at_row // 2 == rank, 1.0, 0.0).astype(BF16)
        keys = keys + lax.dot_general(
            named.astype(BF16), place, (((1,), (1,)), ((), ())), preferred_element_type=F32
        )
    copy = pltpu.make_async_copy(slot_vector, slot, sem)
    copy.start()
    out[...] = jnp.zeros(out.shape, BF16)
    upper = lax.broadcasted_iota(jnp.int32, (2, lanes), 0) == 0
    for d in range(devices):
        both = jnp.where(upper, jnp.broadcast_to(keys[d : d + 1, :], (2, lanes)), 0.0)
        out[d * units + capacity] = both.astype(BF16)
    copy.wait()

    def place_row(turn, carry):
        for i in range(lanes):
            out[slot[turn, i]] = misfit[turn * lanes + i]
        return carry

    lax.fori_loop(0, turns, place_row, 0)


def pack_blocks(misfit, block_tile, block_row, devices):
    count, _, cols = misfit.shape
    capacity = 2 * count // devices
    units = capacity + PAD_UNITS
    grid_shape = (count // cols, cols)
    packed = pl.pallas_call(
        functools.partial(pack_kernel, devices, capacity, units),
        in_specs=vmem_specs(3),
        out_specs=pl.BlockSpec(memory_space=pltpu.VMEM),
        out_shape=jax.ShapeDtypeStruct((devices * units, 2, cols), BF16),
        scratch_shapes=[
            pltpu.VMEM(grid_shape, jnp.int32),
            pltpu.SMEM(grid_shape, jnp.int32),
            pltpu.SemaphoreType.DMA,
        ],
        name="pack_blocks",
    )(block_tile.reshape(grid_shape), block_row.reshape(grid_shape), misfit)
    return packed.reshape(devices * units * 2, cols)


def surface_kernel(devices, capacity, units, got, surface, low, high):
    rows, lanes = surface.shape[1:]
    span = 2 * capacity
    group = max(1, lanes // span)
    at_row = lax.broadcasted_iota(jnp.int32, (2 * rows, lanes), 0).astype(F32)
    odd = (lax.broadcasted_iota(jnp.int32, (1, lanes), 1) % 2).astype(F32) * rows
    total = jnp.zeros((2 * rows, lanes), F32)
    for first in range(0, devices, group):
        key = None
        values = []
        for q in range(group):
            start = (first + q) * units * 2
            tile = got[start + span : start + span + 8, :].astype(F32)[:1, :]
            tile = pltpu.roll(tile, q * span, 1) if q else tile
            key = tile if key is None else key + tile
            values.append(got[start : start + span, :])
        wanted = jnp.where(key > 0.0, key - 1.0 + odd, -1.0)
        select = jnp.where(at_row == wanted, 1.0, 0.0).astype(BF16)
        block = values[0] if group == 1 else jnp.concatenate(values, axis=0)
        total = total + jnp.dot(select, block, preferred_element_type=F32)
    for c in range(2):
        surface[c] = total[c * rows : (c + 1) * rows]
    low[...] = jnp.zeros(low.shape, F32)
    high[...] = jnp.zeros(high.shape, F32)
    for c in range(2):
        low[2 * c : 2 * c + 2, :] = surface[c, :2, :]
        high[2 * c : 2 * c + 2, :] = surface[c, rows - 2 :, :]


def sum_blocks(got, devices, capacity, rows):
    cols = got.shape[1]
    edge = jax.ShapeDtypeStruct((8, cols), F32)
    return pl.pallas_call(
        functools.partial(surface_kernel, devices, capacity, capacity + PAD_UNITS),
        in_specs=vmem_specs(1),
        out_specs=vmem_specs(3),
        out_shape=[jax.ShapeDtypeStruct((2, rows, cols), F32), edge, edge],
        name="sum_blocks",
    )(got)


def source_kernel(surface, above, below, source, packed):
    rows, cols = surface.shape[1:]
    circle = rows + 8
    for c in range(2):
        source[c, :rows, :] = surface[c]
        source[c, rows : rows + 2, :] = below[2 * c : 2 * c + 2, :]
        source[c, rows + 2 : circle - 2, :] = jnp.zeros((4, cols), F32)
        source[c, circle - 2 : circle, :] = above[2 * c : 2 * c + 2, :]
    lane = lane_index((circle, cols))
    first = jnp.where(lane < GROUP, lanes_before(source[0], HALO), 0.0)
    both = jnp.where(lane // GROUP == 1, lanes_before(source[1], HALO + GROUP), first)
    packed[...] = both


def source_columns(surface, above, below):
    _, rows, cols = surface.shape
    circle = rows + 8
    return pl.pallas_call(
        source_kernel,
        in_specs=vmem_specs(3),
        out_specs=vmem_specs(2),
        out_shape=[
            jax.ShapeDtypeStruct((2, circle, cols), F32),
            jax.ShapeDtypeStruct((circle, cols), F32),
        ],
        name="source_columns",
    )(surface, above, below)


def response_kernel(
    source, packed, packed_left, packed_right, scale, eta_in, strip_in, adj_in,
    out, fields, products, eta,
):
    circle, cols = packed.shape
    rows = out.shape[2]
    lane = lane_index((circle, cols))
    column = lane % GROUP
    omegas = omega_list(ITERS)
    zero = jnp.zeros((circle, cols), F32)
    top = lane < GROUP

    strips = []
    for side in range(2):
        if side == 0:
            both = jnp.where(column < HALO, packed_left[...], packed[...])
        else:
            both = jnp.where(column < HALO, packed[...], packed_right[...])
        pair = (jnp.where(top, both, 0.0), jnp.where(top, lanes_after(both, GROUP), 0.0))
        strips.append((strip_in[side, 0], (strip_in[side, 1], strip_in[side, 2]), pair))
    states = [
        [(0.5 * omegas[0]) * (weight[c] * pair[c]) for c in range(2)] for _, weight, pair in strips
    ]
    near = []
    for turn in range(1, ITERS):
        omega = omegas[turn] if turn < ITERS - 1 else None
        left, lows, _ = strip_step(strips[0][0], strips[0][1], states[0], omega, strips[0][2])
        right, _, highs = strip_step(strips[1][0], strips[1][1], states[1], omega, strips[1][2])
        near.append(
            (
                [joined(states[0][c], states[1][c], column) for c in range(2)],
                [joined(lows[c], highs[c], column) for c in range(2)],
            )
        )
        states = [left, right]

    eta[0] = zero
    for k in range(ITERS + 1):
        eta[k + 1] = eta_in[k]
    for half in range(2):
        for c in range(2):
            for k in range(ITERS + 2):
                fields[half, c, k] = zero
                products[half, c, k] = zero
    drive = [0.5 * source[c] for c in range(2)]
    for c in range(2):
        f = omegas[0] * (scale[c, 0] * drive[c])
        fields[0, c, 1] = f
        products[0, c, 1] = eta[1] * f
    for turn in range(1, ITERS):
        half, final = (turn - 1) % 2, turn == ITERS - 1
        edges, sums = near[turn - 1]
        for k in range(turn + 1):
            pair = plane_step(
                k, lane, eta, fields.at[half], products.at[half], scale, edges, sums,
                omegas[turn], drive if k == 0 else None,
            )
            for c in range(2):
                if final:
                    out[c, k] = adj_in[c, k] + pair[c][:rows]
                else:
                    fields[1 - half, c, k + 1] = pair[c]
                    products[1 - half, c, k + 1] = eta[k + 1] * pair[c]


def add_response(source, packed, left, right, scale, eta, strips, adjoint):
    circle, cols = packed.shape
    _, layers, rows, _ = adjoint.shape
    plane = (circle, cols)
    top = pl.BlockSpec((2, ITERS, rows, cols), lambda i: (0, 0, 0, 0))

    def whole(array):
        return pl.BlockSpec(array.shape, lambda i, n=array.ndim: (0,) * n)

    operands = (source, packed, left, right, scale, eta, strips)
    return pl.pallas_call(
        response_kernel,
        grid=(1,),
        in_specs=[whole(array) for array in operands] + [top],
        out_specs=top,
        out_shape=jax.ShapeDtypeStruct(adjoint.shape, F32),
        scratch_shapes=[
            pltpu.VMEM((2, 2, ITERS + 2) + plane, F32),
            pltpu.VMEM((2, 2, ITERS + 2) + plane, F32),
            pltpu.VMEM((ITERS + 2,) + plane, F32),
        ],
        input_output_aliases={7: 0},
        name="add_response",
    )(*operands, adjoint)


def on_device(
    adjoint_prev, viscosity, friction, basal_velocity, ice_mask, misfit, block_tile, block_row
):
    devices = lax.axis_size("gx") * lax.axis_size("gy")
    layers, rows, cols = adjoint_prev.shape[1:]
    capacity = 2 * misfit.shape[0] // devices
    assert layers > 2 * ITERS and GROUP * (layers + 1) <= cols and rows % 8 == 0
    assert 2 * capacity <= cols and cols % (2 * capacity) == 0 and misfit.shape[0] % cols == 0

    edge_low, edge_high = edge_rows(adjoint_prev, viscosity, friction, ice_mask)
    above = shift_up(edge_high, "gx")
    below = shift_down(edge_low, "gx")
    sent = pack_blocks(misfit, block_tile, block_row, devices)
    got = lax.all_to_all(
        sent.reshape(devices, -1, cols), ("gx", "gy"), split_axis=0, concat_axis=0, tiled=True
    )
    u, v, e, f, packed = edge_columns(
        adjoint_prev, viscosity, friction, ice_mask, above, below
    )
    left = shift_up(packed, "gy")
    right = shift_down(packed, "gy")
    adjoint, gradient, scale, eta, strips = free_sweeps(
        u, v, e, f, packed, left, right, basal_velocity
    )
    surface, low, high = sum_blocks(got.reshape(-1, cols), devices, capacity, rows)
    source, source_packed = source_columns(
        surface, shift_up(high, "gx"), shift_down(low, "gx")
    )
    source_left = shift_up(source_packed, "gy")
    source_right = shift_down(source_packed, "gy")
    adjoint = add_response(
        source, source_packed, source_left, source_right, scale, eta, strips, adjoint
    )
    return (adjoint, gradient)


def solution(mesh):
    placed = (
        P(None, None, "gx", "gy"),
        P(None, "gx", "gy"),
        P("gx", "gy"),
        P(None, "gx", "gy"),
        P("gx", "gy"),
        P(("gx", "gy"), None, None),
        P(("gx", "gy"), None),
        P(("gx", "gy")),
    )
    return jax.shard_map(
        on_device,
        mesh=mesh,
        in_specs=placed,
        out_specs=(P(None, None, "gx", "gy"), P("gx", "gy")),
        check_vma=False,
    )
```

time: 177 us -> 85.6 us (0.48)
  other arithmetic: 64.6 us -> 0 us
  local copies, waits for them, and re-layouts: 50.8 us -> 3.51 us
  Pallas kernels: 0 us -> 39 us
  starting transfers between devices: 48.7 us -> 26.1 us
  waiting for transfers between devices: 4.43 us -> 15.5 us
  matrix products: 5.1 us -> 0 us
    pallas_call x0 -> x7, Pallas kernels: none -> 39 us  [the longest x1 21.3 us: free_sweeps(): pl.pallas_call(functools.partial(sweep_kernel, layers), in_specs=vmem_spe...]
    slice x16 -> x0, local copies, waits for them, and re-layouts: 25 us -> none  [the longest x8 13.1 us: with_halo(): last = lax.slice_in_dim(array, length - width, length, axis=dim)]
    another operation x10 -> x0, other arithmetic: 23.1 us -> none  [the longest x6 12.6 us: operate(): return jnp.stack([first, second])]
    mul x13 -> x0, other arithmetic: 18.8 us -> none  [the longest x4 9.51 us: mixed(): flux_x = weight_x * padded_eta[:, :, 1:-1] * along_y]
    ppermute x12 -> x8, starting transfers between devices: 34.9 us -> 19 us  [the longest x4 12.6 us: shift_up(): return lax.ppermute(array, axis, [(i, i + 1) for i in range(peers - 1)])]
    ppermute x6 -> x0, local copies, waits for them, and re-layouts: 11.4 us -> none  [the longest x3 6.43 us: with_halo(): after = lax.ppermute(initial, axis, down)]
    concatenate x6 -> x0, other arithmetic: 11.3 us -> none  [with_halo(): array = jnp.concatenate([before, array, after], axis=dim)]
    ppermute x12 -> x8, waiting for transfers between devices: 4.43 us -> 12.5 us  [the longest x4 9.51 us: shift_down(): return lax.ppermute(array, axis, [(i + 1, i) for i in range(peers - 1)])]
  transfers between devices with their start and end apart: 14 -> 9, of which waited for: 3 -> 4; matrix products, arithmetic and copies ran while one was open for 40% -> 0% of each run, Pallas kernels for 0% -> 36%
where the time goes in v1:
time: 85.6 us; the launch traced here: 84.9 us
  Pallas kernels  39 us (46%)
  starting transfers between devices  26.1 us (30%)
  waiting for transfers between devices  15.5 us (18%)
  local copies, waits for them, and re-layouts  3.51 us (4%)
    pallas_call x1, Pallas kernels, free_sweeps(): pl.pallas_call(functools.partial(sweep_kernel, layers), in_specs=vmem_spe...  21.3 us
    ppermute x4, starting transfers between devices, shift_up(): return lax.ppermute(array, axis, [(i, i + 1) for i in range(peers - 1)])  12.6 us
    ppermute x4, waiting for transfers between devices, shift_down(): return lax.ppermute(array, axis, [(i + 1, i) for i in range(peers - 1)])  9.51 us
    all_to_all x1, starting transfers between devices, on_device(): lax.all_to_all(sent.reshape(devices, -1, cols), ('gx', 'gy'), split_axis=...  7.09 us
    ppermute x4, starting transfers between devices, shift_down(): return lax.ppermute(array, axis, [(i + 1, i) for i in range(peers - 1)])  6.42 us
    pallas_call x1, Pallas kernels, pack_blocks(): pl.pallas_call(functools.partial(pack_kernel, devices, capacity, units),...  4.55 us
    pallas_call x1, Pallas kernels, add_response(): pl.pallas_call(response_kernel, grid=(1,), in_specs=[whole(array) for arr...  3.97 us
    unnamed x18, local copies, waits for them, and re-layouts  3.51 us
  transfers between devices with their start and end apart: 9, of which 4 were waited for; matrix products, arithmetic and copies ran while one was open for 0% of the time, Pallas kernels for 36%

profile of v1, /device:TPU:1, one launch (start us, length us, event | category | flops | bytes accessed | tf_op | source)
XLA Modules:
  0.0 84.9 jit_solution(8872796380500874835)
XLA Ops:
  0.6 4.6 %pack_blocks.1 = bf16[2176,2,128]{2,1,0:T(2,128)(2,1)} custom-call(s32[8,128]{1,0:T(8,128)} %bitcast.6, s32[8,128]{1,0:T(8,128)} %bitcast.7, bf16[1024,2,128]{2,1,0:T(2,128)(2,1)} %misfit.1), custom_call_target="tpu_custom_call" | custom-call | tf_op jit(solution)/shard_map/pack_blocks/pallas_call | solution.py:459
  5.2 7.1 %all-to-all-start = ((bf16[32,136,128]{2,1,0:T(8,128)(2,1)}), bf16[32,136,128]{2,1,0:T(8,128)(2,1)S(1)}, u32[]{:S(2)}, u32[]{:S(2)}) async-start(bf16[32,136,128]{2,1,0:T(8,128)(2,1)} %bitcast.5), calls=%async_computation | async-start | bytes 2228224 | tf_op jit(solution)/shard_map/all_to_all | solution.py:648
  12.3 1.8 %edge_rows.1 = (f32[184,128]{1,0:T(8,128)}, f32[184,128]{1,0:T(8,128)}) custom-call(f32[2,20,64,128]{3,2,1,0:T(8,128)} %adj.1, f32[2,20,64,128]{3,2,1,0:T(8,128)} %adj.1, f32[20,64,128]{2,1,0:T(8,128)} %eta.1, f32[20,64,128]{2,1,0:T(8,128)} %eta.1, f32[64,128]{1,0:T(8,128)} %fr.1, f32[64,128]{1,0:T(8,128)} %fr.1, s32[64,128]{1,0:T(8,128)} %ice.1, s32[64,128]{1,0:T(8,128)} %ice.1), custom_call_target="tpu_custom_call" | custom-call | tf_op jit(solution)/shard_map/edge_rows/pallas_call | solution.py:95
  14.1 3.2 %collective-permute-start.4 = (f32[184,128]{1,0:T(8,128)}, f32[184,128]{1,0:T(8,128)S(1)}, u32[]{:S(2)}, u32[]{:S(2)}) collective-permute-start(f32[184,128]{1,0:T(8,128)} %get-tuple-element.24), channel_id=1, source_target_pairs={{0,8},{8,16},{16,24},{1,9},{9,17},{17,25},{2,10},{10,18},{18,26},{... | collective-permute-start | bytes 282632 | tf_op jit(solution)/shard_map/ppermute | solution.py:30
  17.4 1.3 %collective-permute-start.5 = (f32[184,128]{1,0:T(8,128)}, f32[184,128]{1,0:T(8,128)S(1)}, u32[]{:S(2)}, u32[]{:S(2)}) collective-permute-start(f32[184,128]{1,0:T(8,128)} %get-tuple-element.25), channel_id=1, source_target_pairs={{8,0},{16,8},{24,16},{9,1},{17,9},{25,17},{10,2},{18,10},{26,18},{... | collective-permute-start | bytes 282632 | tf_op jit(solution)/shard_map/ppermute | solution.py:35
  18.7 3.0 %collective-permute-done.4.above = f32[184,128]{1,0:T(8,128)S(1)} collective-permute-done((f32[184,128]{1,0:T(8,128)}, f32[184,128]{1,0:T(8,128)S(1)}, u32[]{:S(2)}, u32[]{:S(2)}) %collective-permute-start.4) | collective-permute-done | bytes 94240 | tf_op jit(solution)/shard_map/ppermute | solution.py:30
  21.7 0.0 copy-start.3
  21.7 6.3 %collective-permute-done.5.below = f32[184,128]{1,0:T(8,128)S(1)} collective-permute-done((f32[184,128]{1,0:T(8,128)}, f32[184,128]{1,0:T(8,128)S(1)}, u32[]{:S(2)}, u32[]{:S(2)}) %collective-permute-start.5) | collective-permute-done | bytes 94240 | tf_op jit(solution)/shard_map/ppermute | solution.py:35
  27.9 0.0 copy-done.3
  27.9 0.0 copy-start.4
  27.9 0.6 copy-done.4
  28.6 3.5 %edge_columns.1 = (f32[20,72,128]{2,1,0:T(8,128)}, f32[20,72,128]{2,1,0:T(8,128)}, f32[20,72,128]{2,1,0:T(8,128)}, f32[72,128]{1,0:T(8,128)}, f32[3,72,128]{2,1,0:T(8,128)}) custom-call(f32[2,20,64,128]{3,2,1,0:T(8,128)} %adj.1, f32[20,64,128]{2,1,0:T(8,128)} %eta.1, f32[64,128]{1,0:T(8,128)} %fr.1, s32[64,128]{1,0:T(8,128)} %ice.1, f32[184,128]{1,0:T(8,128)} %copy-done.3, ...), custom_call_target="tpu_custom_call" | custom-call | tf_op jit(solution)/shard_map/edge_columns/pallas_call | solution.py:142
  32.0 3.7 %collective-permute-start.6 = (f32[3,72,128]{2,1,0:T(8,128)}, f32[3,72,128]{2,1,0:T(8,128)S(1)}, u32[]{:S(2)}, u32[]{:S(2)}) collective-permute-start(f32[3,72,128]{2,1,0:T(8,128)} %get-tuple-element.30.packed), channel_id=1, source_target_pairs={{0,1},{1,2},{2,3},{3,4},{4,5},{5,6},{6,7},{8,9},{9,10},{10,11},{11... | collective-permute-start | bytes 331784 | tf_op jit(solution)/shard_map/ppermute | solution.py:30
  35.7 1.9 %collective-permute-start.7 = (f32[3,72,128]{2,1,0:T(8,128)}, f32[3,72,128]{2,1,0:T(8,128)S(1)}, u32[]{:S(2)}, u32[]{:S(2)}) collective-permute-start(f32[3,72,128]{2,1,0:T(8,128)} %get-tuple-element.30.packed), channel_id=1, source_target_pairs={{1,0},{2,1},{3,2},{4,3},{5,4},{6,5},{7,6},{9,8},{10,9},{11,10},{12... | collective-permute-start | bytes 331784 | tf_op jit(solution)/shard_map/ppermute | solution.py:35
  37.7 3.0 %all-to-all-done = bf16[32,136,128]{2,1,0:T(8,128)(2,1)S(1)} async-done(((bf16[32,136,128]{2,1,0:T(8,128)(2,1)}), bf16[32,136,128]{2,1,0:T(8,128)(2,1)S(1)}, u32[]{:S(2)}, u32[]{:S(2)}) %all-to-all-start) | async-done | bytes 1114144 | tf_op jit(solution)/shard_map/all_to_all | solution.py:648
  40.7 0.0 copy-start
  40.7 1.0 %copy-done = bf16[32,136,128]{2,1,0:T(8,128)(2,1)} copy-done((bf16[32,136,128]{2,1,0:T(8,128)(2,1)}, bf16[32,136,128]{2,1,0:T(8,128)(2,1)S(1)}, u32[]{:S(2)}) %copy-start) | copy-done | bytes 1114136
  41.7 2.3 %sum_blocks.1 = (f32[2,64,128]{2,1,0:T(8,128)}, f32[8,128]{1,0:T(8,128)}, f32[8,128]{1,0:T(8,128)}) custom-call(bf16[4352,128]{1,0:T(8,128)(2,1)} %bitcast.4), custom_call_target="tpu_custom_call" | custom-call | tf_op jit(solution)/shard_map/sum_blocks/pallas_call | solution.py:506
  44.0 2.9 %collective-permute-start = (f32[8,128]{1,0:T(8,128)}, f32[8,128]{1,0:T(8,128)S(1)}, u32[]{:S(2)}, u32[]{:S(2)}) collective-permute-start(f32[8,128]{1,0:T(8,128)} %get-tuple-element.20), channel_id=1, source_target_pairs={{0,8},{8,16},{16,24},{1,9},{9,17},{17,25},{2,10},{10,18},{18,26},{... | collective-permute-start | bytes 12296 | tf_op jit(solution)/shard_map/ppermute | solution.py:30
  46.9 1.3 %collective-permute-start.1 = (f32[8,128]{1,0:T(8,128)}, f32[8,128]{1,0:T(8,128)S(1)}, u32[]{:S(2)}, u32[]{:S(2)}) collective-permute-start(f32[8,128]{1,0:T(8,128)} %get-tuple-element.21), channel_id=1, source_target_pairs={{8,0},{16,8},{24,16},{9,1},{17,9},{25,17},{10,2},{18,10},{26,18},{... | collective-permute-start | bytes 12296 | tf_op jit(solution)/shard_map/ppermute | solution.py:35
  48.2 0.0 collective-permute-done.above
  48.2 0.0 copy-start.7
  48.2 3.2 %collective-permute-done.1.below = f32[8,128]{1,0:T(8,128)S(1)} collective-permute-done((f32[8,128]{1,0:T(8,128)}, f32[8,128]{1,0:T(8,128)S(1)}, u32[]{:S(2)}, u32[]{:S(2)}) %collective-permute-start.1) | collective-permute-done | bytes 4128 | tf_op jit(solution)/shard_map/ppermute | solution.py:35
  51.4 0.0 copy-start.8
  51.4 0.0 copy-done.7
  51.4 0.6 copy-done.8
  52.0 1.6 %source_columns.1 = (f32[2,72,128]{2,1,0:T(8,128)}, f32[72,128]{1,0:T(8,128)}) custom-call(f32[2,64,128]{2,1,0:T(8,128)} %get-tuple-element.19.surface, f32[8,128]{1,0:T(8,128)} %copy-done.7, f32[8,128]{1,0:T(8,128)} %copy-done.8), custom_call_target="tpu_custom_call" | custom-call | tf_op jit(solution)/shard_map/source_columns/pallas_call | solution.py:532
  53.6 2.7 %collective-permute-start.2 = (f32[72,128]{1,0:T(8,128)}, f32[72,128]{1,0:T(8,128)S(1)}, u32[]{:S(2)}, u32[]{:S(2)}) collective-permute-start(f32[72,128]{1,0:T(8,128)} %get-tuple-element.23.packed), channel_id=1, source_target_pairs={{0,1},{1,2},{2,3},{3,4},{4,5},{5,6},{6,7},{8,9},{9,10},{10,11},{11... | collective-permute-start | bytes 110600 | tf_op jit(solution)/shard_map/ppermute | solution.py:30
  56.4 1.9 %collective-permute-start.3 = (f32[72,128]{1,0:T(8,128)}, f32[72,128]{1,0:T(8,128)S(1)}, u32[]{:S(2)}, u32[]{:S(2)}) collective-permute-start(f32[72,128]{1,0:T(8,128)} %get-tuple-element.23.packed), channel_id=1, source_target_pairs={{1,0},{2,1},{3,2},{4,3},{5,4},{6,5},{7,6},{9,8},{10,9},{11,10},{12... | collective-permute-start | bytes 110600 | tf_op jit(solution)/shard_map/ppermute | solution.py:35
  58.3 0.0 collective-permute-done.6.packed_left
  58.3 0.0 copy-start.1
  58.3 0.0 collective-permute-done.7.packed_right
  58.3 0.0 copy-start.2
  58.3 0.6 copy-done.1
  58.9 0.1 copy-done.2
  59.0 21.3 %free_sweeps.1 = (f32[2,20,64,128]{3,2,1,0:T(8,128)}, f32[64,128]{1,0:T(8,128)}, f32[2,3,72,128]{3,2,1,0:T(8,128)}, f32[4,72,128]{2,1,0:T(8,128)}, f32[2,3,72,128]{3,2,1,0:T(8,128)}) custom-call(f32[20,72,128]{2,1,0:T(8,128)} %get-tuple-element.26.u_in, f32[20,72,128]{2,1,0:T(8,128)} %get-tuple-element.27.v_in, f32[20,72,128]{2,1,0:T(8,128)} %get-tuple-element.28.e_in, ...), custom_call_target="tpu_custom_call" | custom-call | flops 200000000 | bytes 8000000 | tf_op jit(solution)/shard_map/free_sweeps/pallas_call | solution.py:391
  80.3 0.0 collective-permute-done.2.packed_left
  80.3 0.0 copy-start.5
  80.3 0.0 collective-permute-done.3.packed_right
  80.3 0.0 copy-start.6
  80.3 0.6 copy-done.5
  80.9 0.0 copy-done.6
  80.9 4.0 %add_response.1 = f32[2,20,64,128]{3,2,1,0:T(8,128)} custom-call(f32[2,72,128]{2,1,0:T(8,128)} %get-tuple-element.22.source, f32[72,128]{1,0:T(8,128)} %get-tuple-element.23.packed, f32[72,128]{1,0:T(8,128)} %copy-done.5, f32[72,128]{1,0:T(8,128)} %copy-done.6, f32[2,3,72,128]{3,2,1,0:T(8,128)} %get-tuple-element.31.scale, ...), custom_call_target="tpu_custom_call", output_to_operand_aliasing={{}: (7, {})} | custom-call | tf_op jit(solution)/shard_map/add_response/pallas_call | solution.py:619
Async XLA Ops:
  5.2 35.5 %all-to-all-start = ((bf16[32,136,128]{2,1,0:T(8,128)(2,1)}), bf16[32,136,128]{2,1,0:T(8,128)(2,1)S(1)}, u32[]{:S(2)}, u32[]{:S(2)}) async-start(bf16[32,136,128]{2,1,0:T(8,128)(2,1)} %bitcast.5), calls=%async_computation | async-start | bytes 2228224 | tf_op jit(solution)/shard_map/all_to_all | solution.py:648
  14.1 7.5 %collective-permute-start.4 = (f32[184,128]{1,0:T(8,128)}, f32[184,128]{1,0:T(8,128)S(1)}, u32[]{:S(2)}, u32[]{:S(2)}) collective-permute-start(f32[184,128]{1,0:T(8,128)} %get-tuple-element.24), channel_id=1, source_target_pairs={{0,8},{8,16},{16,24},{1,9},{9,17},{17,25},{2,10},{10,18},{18,26},{... | collective-permute-start | bytes 282632 | tf_op jit(solution)/shard_map/ppermute | solution.py:30
  17.4 10.5 %collective-permute-start.5 = (f32[184,128]{1,0:T(8,128)}, f32[184,128]{1,0:T(8,128)S(1)}, u32[]{:S(2)}, u32[]{:S(2)}) collective-permute-start(f32[184,128]{1,0:T(8,128)} %get-tuple-element.25), channel_id=1, source_target_pairs={{8,0},{16,8},{24,16},{9,1},{17,9},{25,17},{10,2},{18,10},{26,18},{... | collective-permute-start | bytes 282632 | tf_op jit(solution)/shard_map/ppermute | solution.py:35
  21.7 6.3 %copy-start.3 = (f32[184,128]{1,0:T(8,128)}, f32[184,128]{1,0:T(8,128)S(1)}, u32[]{:S(2)}) copy-start(f32[184,128]{1,0:T(8,128)S(1)} %collective-permute-done.4.above) | copy-start | bytes 282628
  27.9 0.6 copy-start.4
  32.0 26.3 %collective-permute-start.6 = (f32[3,72,128]{2,1,0:T(8,128)}, f32[3,72,128]{2,1,0:T(8,128)S(1)}, u32[]{:S(2)}, u32[]{:S(2)}) collective-permute-start(f32[3,72,128]{2,1,0:T(8,128)} %get-tuple-element.30.packed), channel_id=1, source_target_pairs={{0,1},{1,2},{2,3},{3,4},{4,5},{5,6},{6,7},{8,9},{9,10},{10,11},{11... | collective-permute-start | bytes 331784 | tf_op jit(solution)/shard_map/ppermute | solution.py:30
  35.7 22.6 %collective-permute-start.7 = (f32[3,72,128]{2,1,0:T(8,128)}, f32[3,72,128]{2,1,0:T(8,128)S(1)}, u32[]{:S(2)}, u32[]{:S(2)}) collective-permute-start(f32[3,72,128]{2,1,0:T(8,128)} %get-tuple-element.30.packed), channel_id=1, source_target_pairs={{1,0},{2,1},{3,2},{4,3},{5,4},{6,5},{7,6},{9,8},{10,9},{11,10},{12... | collective-permute-start | bytes 331784 | tf_op jit(solution)/shard_map/ppermute | solution.py:35
  40.7 1.0 %copy-start = (bf16[32,136,128]{2,1,0:T(8,128)(2,1)}, bf16[32,136,128]{2,1,0:T(8,128)(2,1)S(1)}, u32[]{:S(2)}) copy-start(bf16[32,136,128]{2,1,0:T(8,128)(2,1)S(1)} %all-to-all-done) | copy-start | bytes 3342340
  44.0 4.2 %collective-permute-start = (f32[8,128]{1,0:T(8,128)}, f32[8,128]{1,0:T(8,128)S(1)}, u32[]{:S(2)}, u32[]{:S(2)}) collective-permute-start(f32[8,128]{1,0:T(8,128)} %get-tuple-element.20), channel_id=1, source_target_pairs={{0,8},{8,16},{16,24},{1,9},{9,17},{17,25},{2,10},{10,18},{18,26},{... | collective-permute-start | bytes 12296 | tf_op jit(solution)/shard_map/ppermute | solution.py:30
  46.9 4.6 %collective-permute-start.1 = (f32[8,128]{1,0:T(8,128)}, f32[8,128]{1,0:T(8,128)S(1)}, u32[]{:S(2)}, u32[]{:S(2)}) collective-permute-start(f32[8,128]{1,0:T(8,128)} %get-tuple-element.21), channel_id=1, source_target_pairs={{8,0},{16,8},{24,16},{9,1},{17,9},{25,17},{10,2},{18,10},{26,18},{... | collective-permute-start | bytes 12296 | tf_op jit(solution)/shard_map/ppermute | solution.py:35
  48.2 3.3 %copy-start.7 = (f32[8,128]{1,0:T(8,128)}, f32[8,128]{1,0:T(8,128)S(1)}, u32[]{:S(2)}) copy-start(f32[8,128]{1,0:T(8,128)S(1)} %collective-permute-done.above) | copy-start | bytes 12292
  51.4 0.6 copy-start.8
  53.6 26.7 %collective-permute-start.2 = (f32[72,128]{1,0:T(8,128)}, f32[72,128]{1,0:T(8,128)S(1)}, u32[]{:S(2)}, u32[]{:S(2)}) collective-permute-start(f32[72,128]{1,0:T(8,128)} %get-tuple-element.23.packed), channel_id=1, source_target_pairs={{0,1},{1,2},{2,3},{3,4},{4,5},{5,6},{6,7},{8,9},{9,10},{10,11},{11... | collective-permute-start | bytes 110600 | tf_op jit(solution)/shard_map/ppermute | solution.py:30
  56.4 23.9 %collective-permute-start.3 = (f32[72,128]{1,0:T(8,128)}, f32[72,128]{1,0:T(8,128)S(1)}, u32[]{:S(2)}, u32[]{:S(2)}) collective-permute-start(f32[72,128]{1,0:T(8,128)} %get-tuple-element.23.packed), channel_id=1, source_target_pairs={{1,0},{2,1},{3,2},{4,3},{5,4},{6,5},{7,6},{9,8},{10,9},{11,10},{12... | collective-permute-start | bytes 110600 | tf_op jit(solution)/shard_map/ppermute | solution.py:35
  58.3 0.6 copy-start.1
  58.3 0.7 copy-start.2
  80.3 0.6 copy-start.5
  80.3 0.6 copy-start.6

commit v2 on v1

--- a/solution.py
+++ b/solution.py
@@ -7,6 +7,7 @@
 from jax.experimental import pallas as pl
 from jax.experimental.pallas import tpu as pltpu
 from jax.sharding import PartitionSpec as P
+
 
 ITERS = 3
 HALO = ITERS
@@ -98,6 +99,7 @@
         in_specs=specs,
         out_specs=[pl.BlockSpec((length, cols), lambda i: (0, 0))] * 2,
         out_shape=[jax.ShapeDtypeStruct((length, cols), F32)] * 2,
+        compiler_params=pltpu.CompilerParams(vmem_limit_bytes=4 << 20),
         name="edge_rows",
     )(adjoint, adjoint, viscosity, viscosity, friction, friction, ice_mask, ice_mask)
 
@@ -150,6 +152,7 @@
             jax.ShapeDtypeStruct((circle, cols), F32),
             jax.ShapeDtypeStruct((3, circle, cols), F32),
         ],
+        compiler_params=pltpu.CompilerParams(vmem_limit_bytes=12 << 20),
         name="edge_columns",
     )(adjoint, viscosity, friction, ice_mask, above, below)
 
@@ -410,6 +413,7 @@
         cost_estimate=pl.CostEstimate(
             flops=200_000_000, transcendentals=0, bytes_accessed=8_000_000
         ),
+        compiler_params=pltpu.CompilerParams(vmem_limit_bytes=24 << 20),
         name="free_sweeps",
     )(u, v, e, f, packed, left, right, basal_velocity)
 
@@ -466,6 +470,7 @@
             pltpu.SMEM(grid_shape, jnp.int32),
             pltpu.SemaphoreType.DMA,
         ],
+        compiler_params=pltpu.CompilerParams(vmem_limit_bytes=4 << 20),
         name="pack_blocks",
     )(block_tile.reshape(grid_shape), block_row.reshape(grid_shape), misfit)
     return packed.reshape(devices * units * 2, cols)
@@ -508,6 +513,7 @@
         in_specs=vmem_specs(1),
         out_specs=vmem_specs(3),
         out_shape=[jax.ShapeDtypeStruct((2, rows, cols), F32), edge, edge],
+        compiler_params=pltpu.CompilerParams(vmem_limit_bytes=4 << 20),
         name="sum_blocks",
     )(got)
 
@@ -537,6 +543,7 @@
             jax.ShapeDtypeStruct((2, circle, cols), F32),
             jax.ShapeDtypeStruct((circle, cols), F32),
         ],
+        compiler_params=pltpu.CompilerParams(vmem_limit_bytes=2 << 20),
         name="source_columns",
     )(surface, above, below)
 
@@ -608,7 +615,7 @@
 
 def add_response(source, packed, left, right, scale, eta, strips, adjoint):
     circle, cols = packed.shape
-    _, layers, rows, _ = adjoint.shape
+    _, _, rows, _ = adjoint.shape
     plane = (circle, cols)
     top = pl.BlockSpec((2, ITERS, rows, cols), lambda i: (0, 0, 0, 0))
 
@@ -628,6 +635,7 @@
             pltpu.VMEM((ITERS + 2,) + plane, F32),
         ],
         input_output_aliases={7: 0},
+        compiler_params=pltpu.CompilerParams(vmem_limit_bytes=8 << 20),
         name="add_response",
     )(*operands, adjoint)
 
@@ -679,6 +687,7 @@
         P(("gx", "gy"), None),
         P(("gx", "gy")),
     )
+
     return jax.shard_map(
         on_device,
         mesh=mesh,

time: 85.6 us -> 80.2 us (0.937)
  Pallas kernels: 39 us -> 26.5 us
  local copies, waits for them, and re-layouts: 3.51 us -> 8.27 us
  starting transfers between devices: 26.1 us -> 27.6 us
    unnamed x18 -> x30, local copies, waits for them, and re-layouts: 3.51 us -> 8.27 us
    pallas_call x1, Pallas kernels: 3.47 us -> 0.69 us  [edge_columns(): pl.pallas_call(functools.partial(column_kernel, layers), in_specs=vmem_sp...]
    pallas_call x1, Pallas kernels: 4.55 us -> 1.97 us  [pack_blocks(): pl.pallas_call(functools.partial(pack_kernel, devices, capacity, units),...]
    pallas_call x1, Pallas kernels: 2.3 us -> 0.43 us  [sum_blocks(): pl.pallas_call(functools.partial(surface_kernel, devices, capacity, capac...]
    pallas_call x1, Pallas kernels: 1.85 us -> 0.09 us  [edge_rows(): pl.pallas_call(functools.partial(edge_kernel, layers), grid=(1,), in_spec...]
    pallas_call x1, Pallas kernels: 21.3 us -> 19.6 us  [free_sweeps(): pl.pallas_call(functools.partial(sweep_kernel, layers), in_specs=vmem_spe...]
    pallas_call x1, Pallas kernels: 1.57 us -> 0.08 us  [source_columns(): pl.pallas_call(source_kernel, in_specs=vmem_specs(3), out_specs=vmem_spec...]
    ppermute x4, starting transfers between devices: 12.6 us -> 13.9 us  [shift_up(): return lax.ppermute(array, axis, [(i, i + 1) for i in range(peers - 1)])]
  transfers between devices with their start and end apart: 9 -> 9, of which waited for: 4 -> 4; matrix products, arithmetic and copies ran while one was open for 0% -> 0% of each run, Pallas kernels for 36% -> 26%
where the time goes in v2:
time: 80.2 us; the launch traced here: 79.5 us
  starting transfers between devices  27.6 us (34%)
  Pallas kernels  26.5 us (33%)
  waiting for transfers between devices  16.3 us (20%)
  local copies, waits for them, and re-layouts  8.27 us (10%)
  between operations  0.86 us (1%)
    pallas_call x1, Pallas kernels, free_sweeps(): pl.pallas_call(functools.partial(sweep_kernel, layers), in_specs=vmem_spe...  19.6 us
    ppermute x4, starting transfers between devices, shift_up(): return lax.ppermute(array, axis, [(i, i + 1) for i in range(peers - 1)])  13.9 us
    ppermute x4, waiting for transfers between devices, shift_down(): return lax.ppermute(array, axis, [(i + 1, i) for i in range(peers - 1)])  8.93 us
    unnamed x30, local copies, waits for them, and re-layouts  8.27 us
    all_to_all x1, starting transfers between devices, on_device(): lax.all_to_all(sent.reshape(devices, -1, cols), ('gx', 'gy'), split_axis=...  7.09 us
    ppermute x4, starting transfers between devices, shift_down(): return lax.ppermute(array, axis, [(i + 1, i) for i in range(peers - 1)])  6.56 us
    all_to_all x1, waiting for transfers between devices, on_device(): lax.all_to_all(sent.reshape(devices, -1, cols), ('gx', 'gy'), split_axis=...  3.87 us
    pallas_call x1, Pallas kernels, add_response(): pl.pallas_call(response_kernel, grid=(1,), in_specs=[whole(array) for arr...  3.64 us
  transfers between devices with their start and end apart: 9, of which 4 were waited for; matrix products, arithmetic and copies ran while one was open for 0% of the time, Pallas kernels for 26%

profile of v2, /device:TPU:1, one launch (start us, length us, event | category | flops | bytes accessed | tf_op | source)
XLA Modules:
  0.0 79.5 jit_solution(16961403681113361615)
XLA Ops:
  0.6 0.0 copy-start.9
  0.6 1.0 %copy-done.9 = bf16[1024,2,128]{2,1,0:T(2,128)(2,1)S(1)} copy-done((bf16[1024,2,128]{2,1,0:T(2,128)(2,1)S(1)}, bf16[1024,2,128]{2,1,0:T(2,128)(2,1)}, u32[]{:S(2)}) %copy-start.9) | copy-done | bytes 524312
  1.7 0.0 copy-start.13
  1.7 0.7 copy-done.13
  2.4 0.0 copy-start.14
  2.4 0.7 copy-done.14
  3.0 2.0 %pack_blocks.1 = bf16[2176,2,128]{2,1,0:T(2,128)(2,1)S(1)} custom-call(s32[8,128]{1,0:T(8,128)S(1)} %bitcast.6, s32[8,128]{1,0:T(8,128)S(1)} %bitcast.7, bf16[1024,2,128]{2,1,0:T(2,128)(2,1)S(1)} %copy-done.9), custom_call_target="tpu_custom_call" | custom-call | tf_op jit(solution)/shard_map/pack_blocks/pallas_call | solution.py:463
  5.0 0.0 copy-start.2
  5.0 1.0 %copy-done.2 = bf16[2176,2,128]{2,1,0:T(2,128)(2,1)} copy-done((bf16[2176,2,128]{2,1,0:T(2,128)(2,1)}, bf16[2176,2,128]{2,1,0:T(2,128)(2,1)S(1)}, u32[]{:S(2)}) %copy-start.2) | copy-done | bytes 1114136
  6.0 0.0 copy-start
  6.0 0.0 copy-start.1
  6.0 0.0 copy-start.10
  6.0 0.0 copy-start.11
  6.0 7.1 %all-to-all-start = ((bf16[32,136,128]{2,1,0:T(8,128)(2,1)}), bf16[32,136,128]{2,1,0:T(8,128)(2,1)S(1)}, u32[]{:S(2)}, u32[]{:S(2)}) async-start(bf16[32,136,128]{2,1,0:T(8,128)(2,1)} %bitcast.5), calls=%async_computation | async-start | bytes 2228224 | tf_op jit(solution)/shard_map/all_to_all | solution.py:656
  13.1 0.0 copy-done
  13.1 0.0 copy-done.1
  13.1 0.0 copy-done.10
  13.2 0.0 copy-done.11
  13.2 0.1 edge_rows.1
  13.3 3.3 %collective-permute-start.4 = (f32[184,128]{1,0:T(8,128)S(1)}, f32[184,128]{1,0:T(8,128)S(1)}, u32[]{:S(2)}, u32[]{:S(2)}) collective-permute-start(f32[184,128]{1,0:T(8,128)S(1)} %get-tuple-element.24), channel_id=1, source_target_pairs={{0,8},{8,16},{16,24},{1,9},{9,17},{17,25},{2,10},{10,18},{18,26},{... | collective-permute-start | bytes 282632 | tf_op jit(solution)/shard_map/ppermute | solution.py:31
  16.5 0.0 copy-start.12
  16.5 1.4 %collective-permute-start.5 = (f32[184,128]{1,0:T(8,128)S(1)}, f32[184,128]{1,0:T(8,128)S(1)}, u32[]{:S(2)}, u32[]{:S(2)}) collective-permute-start(f32[184,128]{1,0:T(8,128)S(1)} %get-tuple-element.25), channel_id=1, source_target_pairs={{8,0},{16,8},{24,16},{9,1},{17,9},{25,17},{10,2},{18,10},{26,18},{... | collective-permute-start | bytes 282632 | tf_op jit(solution)/shard_map/ppermute | solution.py:36
  18.0 3.5 %collective-permute-done.4.above = f32[184,128]{1,0:T(8,128)S(1)} collective-permute-done((f32[184,128]{1,0:T(8,128)S(1)}, f32[184,128]{1,0:T(8,128)S(1)}, u32[]{:S(2)}, u32[]{:S(2)}) %collective-permute-start.4) | collective-permute-done | bytes 94240 | tf_op jit(solution)/shard_map/ppermute | solution.py:31
  21.5 5.9 %collective-permute-done.5.below = f32[184,128]{1,0:T(8,128)S(1)} collective-permute-done((f32[184,128]{1,0:T(8,128)S(1)}, f32[184,128]{1,0:T(8,128)S(1)}, u32[]{:S(2)}, u32[]{:S(2)}) %collective-permute-start.5) | collective-permute-done | bytes 94240 | tf_op jit(solution)/shard_map/ppermute | solution.py:36
  27.4 0.7 edge_columns.1
  28.1 0.0 copy-start.3
  28.1 0.9 %copy-done.3 = f32[20,72,128]{2,1,0:T(8,128)} copy-done((f32[20,72,128]{2,1,0:T(8,128)}, f32[20,72,128]{2,1,0:T(8,128)S(1)}, u32[]{:S(2)}) %copy-start.3) | copy-done | bytes 737304
  29.0 0.0 copy-start.5
  29.0 0.9 %copy-done.5 = f32[20,72,128]{2,1,0:T(8,128)} copy-done((f32[20,72,128]{2,1,0:T(8,128)}, f32[20,72,128]{2,1,0:T(8,128)S(1)}, u32[]{:S(2)}) %copy-start.5) | copy-done | bytes 737304
  29.9 0.0 copy-start.7
  29.9 0.9 %copy-done.7 = f32[20,72,128]{2,1,0:T(8,128)} copy-done((f32[20,72,128]{2,1,0:T(8,128)}, f32[20,72,128]{2,1,0:T(8,128)S(1)}, u32[]{:S(2)}) %copy-start.7) | copy-done | bytes 737304
  30.7 0.0 copy-start.4
  30.7 5.0 %collective-permute-start.6 = (f32[3,72,128]{2,1,0:T(8,128)S(1)}, f32[3,72,128]{2,1,0:T(8,128)S(1)}, u32[]{:S(2)}, u32[]{:S(2)}) collective-permute-start(f32[3,72,128]{2,1,0:T(8,128)S(1)} %get-tuple-element.30.packed), channel_id=1, source_target_pairs={{0,1},{1,2},{2,3},{3,4},{4,5},{5,6},{6,7},{8,9},{9,10},{10,11},{11... | collective-permute-start | bytes 331784 | tf_op jit(solution)/shard_map/ppermute | solution.py:31
  35.7 1.9 %collective-permute-start.7 = (f32[3,72,128]{2,1,0:T(8,128)S(1)}, f32[3,72,128]{2,1,0:T(8,128)S(1)}, u32[]{:S(2)}, u32[]{:S(2)}) collective-permute-start(f32[3,72,128]{2,1,0:T(8,128)S(1)} %get-tuple-element.30.packed), channel_id=1, source_target_pairs={{1,0},{2,1},{3,2},{4,3},{5,4},{6,5},{7,6},{9,8},{10,9},{11,10},{12... | collective-permute-start | bytes 331784 | tf_op jit(solution)/shard_map/ppermute | solution.py:36
  37.6 3.9 %all-to-all-done = bf16[32,136,128]{2,1,0:T(8,128)(2,1)S(1)} async-done(((bf16[32,136,128]{2,1,0:T(8,128)(2,1)}), bf16[32,136,128]{2,1,0:T(8,128)(2,1)S(1)}, u32[]{:S(2)}, u32[]{:S(2)}) %all-to-all-start) | async-done | bytes 1114144 | tf_op jit(solution)/shard_map/all_to_all | solution.py:656
  41.5 0.4 sum_blocks.1
  41.9 2.8 %collective-permute-start = (f32[8,128]{1,0:T(8,128)S(1)}, f32[8,128]{1,0:T(8,128)S(1)}, u32[]{:S(2)}, u32[]{:S(2)}) collective-permute-start(f32[8,128]{1,0:T(8,128)S(1)} %get-tuple-element.20), channel_id=1, source_target_pairs={{0,8},{8,16},{16,24},{1,9},{9,17},{17,25},{2,10},{10,18},{18,26},{... | collective-permute-start | bytes 12296 | tf_op jit(solution)/shard_map/ppermute | solution.py:31
  44.8 1.3 %collective-permute-start.1 = (f32[8,128]{1,0:T(8,128)S(1)}, f32[8,128]{1,0:T(8,128)S(1)}, u32[]{:S(2)}, u32[]{:S(2)}) collective-permute-start(f32[8,128]{1,0:T(8,128)S(1)} %get-tuple-element.21), channel_id=1, source_target_pairs={{8,0},{16,8},{24,16},{9,1},{17,9},{25,17},{10,2},{18,10},{26,18},{... | collective-permute-start | bytes 12296 | tf_op jit(solution)/shard_map/ppermute | solution.py:36
  46.1 0.0 collective-permute-done.above
  46.1 3.0 %collective-permute-done.1.below = f32[8,128]{1,0:T(8,128)S(1)} collective-permute-done((f32[8,128]{1,0:T(8,128)S(1)}, f32[8,128]{1,0:T(8,128)S(1)}, u32[]{:S(2)}, u32[]{:S(2)}) %collective-permute-start.1) | collective-permute-done | bytes 4128 | tf_op jit(solution)/shard_map/ppermute | solution.py:36
  49.1 0.1 source_columns.1
  49.2 2.9 %collective-permute-start.2 = (f32[72,128]{1,0:T(8,128)S(1)}, f32[72,128]{1,0:T(8,128)S(1)}, u32[]{:S(2)}, u32[]{:S(2)}) collective-permute-start(f32[72,128]{1,0:T(8,128)S(1)} %get-tuple-element.23.packed), channel_id=1, source_target_pairs={{0,1},{1,2},{2,3},{3,4},{4,5},{5,6},{6,7},{8,9},{9,10},{10,11},{11... | collective-permute-start | bytes 110600 | tf_op jit(solution)/shard_map/ppermute | solution.py:31
  52.1 1.9 %collective-permute-start.3 = (f32[72,128]{1,0:T(8,128)S(1)}, f32[72,128]{1,0:T(8,128)S(1)}, u32[]{:S(2)}, u32[]{:S(2)}) collective-permute-start(f32[72,128]{1,0:T(8,128)S(1)} %get-tuple-element.23.packed), channel_id=1, source_target_pairs={{1,0},{2,1},{3,2},{4,3},{5,4},{6,5},{7,6},{9,8},{10,9},{11,10},{12... | collective-permute-start | bytes 110600 | tf_op jit(solution)/shard_map/ppermute | solution.py:36
  54.0 0.0 collective-permute-done.6.packed_left
  54.0 0.0 collective-permute-done.7.packed_right
  54.0 0.0 copy-done.12
  54.0 0.0 copy-done.4
  54.1 0.0 copy-start.6
  54.1 1.1 %copy-done.6 = f32[20,72,128]{2,1,0:T(8,128)S(1)} copy-done((f32[20,72,128]{2,1,0:T(8,128)S(1)}, f32[20,72,128]{2,1,0:T(8,128)}, u32[]{:S(2)}) %copy-start.6) | copy-done | bytes 737304
  55.2 0.0 copy-start.8
  55.2 1.1 %copy-done.8 = f32[20,72,128]{2,1,0:T(8,128)S(1)} copy-done((f32[20,72,128]{2,1,0:T(8,128)S(1)}, f32[20,72,128]{2,1,0:T(8,128)}, u32[]{:S(2)}) %copy-start.8) | copy-done | bytes 737304
  56.3 19.6 %free_sweeps.1 = (f32[2,20,64,128]{3,2,1,0:T(8,128)}, f32[64,128]{1,0:T(8,128)}, f32[2,3,72,128]{3,2,1,0:T(8,128)S(1)}, f32[4,72,128]{2,1,0:T(8,128)S(1)}, f32[2,3,72,128]{3,2,1,0:T(8,128)S(1)}) custom-call(f32[20,72,128]{2,1,0:T(8,128)S(1)} %copy-done.4, f32[20,72,128]{2,1,0:T(8,128)S(1)} %copy-done.6, f32[20,72,128]{2,1,0:T(8,128)S(1)} %copy-done.8, ...), custom_call_target="tpu_custom_call" | custom-call | flops 200000000 | bytes 8000000 | tf_op jit(solution)/shard_map/free_sweeps/pallas_call | solution.py:394
  75.9 0.0 collective-permute-done.2.packed_left
  75.9 0.0 collective-permute-done.3.packed_right
  75.9 3.6 %add_response.1 = f32[2,20,64,128]{3,2,1,0:T(8,128)} custom-call(f32[2,72,128]{2,1,0:T(8,128)S(1)} %get-tuple-element.22.source, f32[72,128]{1,0:T(8,128)S(1)} %get-tuple-element.23.packed, f32[72,128]{1,0:T(8,128)S(1)} %collective-permute-done.2.packed_left, f32[72,128]{1,0:T(8,128)S(1)} %collective-permute-done.3.packed_right, ...), custom_call_target="tpu_custom_call", output_to_operand_aliasing={{}: (7, {})} | custom-call | tf_op jit(solution)/shard_map/add_response/pallas_call | solution.py:626
Async XLA Ops:
  0.6 1.0 %copy-start.9 = (bf16[1024,2,128]{2,1,0:T(2,128)(2,1)S(1)}, bf16[1024,2,128]{2,1,0:T(2,128)(2,1)}, u32[]{:S(2)}) copy-start(bf16[1024,2,128]{2,1,0:T(2,128)(2,1)} %misfit.1) | copy-start | bytes 1572868
  1.7 0.7 copy-start.13
  2.4 0.7 copy-start.14
  5.0 1.0 %copy-start.2 = (bf16[2176,2,128]{2,1,0:T(2,128)(2,1)}, bf16[2176,2,128]{2,1,0:T(2,128)(2,1)S(1)}, u32[]{:S(2)}) copy-start(bf16[2176,2,128]{2,1,0:T(2,128)(2,1)S(1)} %pack_blocks.1) | copy-start | bytes 3342340
  6.0 7.1 %copy-start = (f32[2,20,64,128]{3,2,1,0:T(8,128)S(1)}, f32[2,20,64,128]{3,2,1,0:T(8,128)}, u32[]{:S(2)}) copy-start(f32[2,20,64,128]{3,2,1,0:T(8,128)} %adj.1) | copy-start | bytes 3932164
  6.0 7.1 %copy-start.1 = (f32[20,64,128]{2,1,0:T(8,128)S(1)}, f32[20,64,128]{2,1,0:T(8,128)}, u32[]{:S(2)}) copy-start(f32[20,64,128]{2,1,0:T(8,128)} %eta.1) | copy-start | bytes 1966084
  6.0 7.1 %copy-start.10 = (f32[64,128]{1,0:T(8,128)S(1)}, f32[64,128]{1,0:T(8,128)}, u32[]{:S(2)}) copy-start(f32[64,128]{1,0:T(8,128)} %fr.1) | copy-start | bytes 98308
  6.0 7.1 %copy-start.11 = (s32[64,128]{1,0:T(8,128)S(1)}, s32[64,128]{1,0:T(8,128)}, u32[]{:S(2)}) copy-start(s32[64,128]{1,0:T(8,128)} %ice.1) | copy-start | bytes 98308
  6.0 35.5 %all-to-all-start = ((bf16[32,136,128]{2,1,0:T(8,128)(2,1)}), bf16[32,136,128]{2,1,0:T(8,128)(2,1)S(1)}, u32[]{:S(2)}, u32[]{:S(2)}) async-start(bf16[32,136,128]{2,1,0:T(8,128)(2,1)} %bitcast.5), calls=%async_computation | async-start | bytes 2228224 | tf_op jit(solution)/shard_map/all_to_all | solution.py:656
  13.3 8.2 %collective-permute-start.4 = (f32[184,128]{1,0:T(8,128)S(1)}, f32[184,128]{1,0:T(8,128)S(1)}, u32[]{:S(2)}, u32[]{:S(2)}) collective-permute-start(f32[184,128]{1,0:T(8,128)S(1)} %get-tuple-element.24), channel_id=1, source_target_pairs={{0,8},{8,16},{16,24},{1,9},{9,17},{17,25},{2,10},{10,18},{18,26},{... | collective-permute-start | bytes 282632 | tf_op jit(solution)/shard_map/ppermute | solution.py:31
  16.5 37.5 %copy-start.12 = (f32[2,64,128]{2,1,0:T(8,128)S(1)}, f32[2,64,128]{2,1,0:T(8,128)}, u32[]{:S(2)}) copy-start(f32[2,64,128]{2,1,0:T(8,128)} %basal_velocity.1) | copy-start | bytes 196612
  16.5 10.8 %collective-permute-start.5 = (f32[184,128]{1,0:T(8,128)S(1)}, f32[184,128]{1,0:T(8,128)S(1)}, u32[]{:S(2)}, u32[]{:S(2)}) collective-permute-start(f32[184,128]{1,0:T(8,128)S(1)} %get-tuple-element.25), channel_id=1, source_target_pairs={{8,0},{16,8},{24,16},{9,1},{17,9},{25,17},{10,2},{18,10},{26,18},{... | collective-permute-start | bytes 282632 | tf_op jit(solution)/shard_map/ppermute | solution.py:36
  28.1 0.9 %copy-start.3 = (f32[20,72,128]{2,1,0:T(8,128)}, f32[20,72,128]{2,1,0:T(8,128)S(1)}, u32[]{:S(2)}) copy-start(f32[20,72,128]{2,1,0:T(8,128)S(1)} %get-tuple-element.26.u_in) | copy-start | bytes 2211844
  29.0 0.9 %copy-start.5 = (f32[20,72,128]{2,1,0:T(8,128)}, f32[20,72,128]{2,1,0:T(8,128)S(1)}, u32[]{:S(2)}) copy-start(f32[20,72,128]{2,1,0:T(8,128)S(1)} %get-tuple-element.27.v_in) | copy-start | bytes 2211844
  29.9 0.9 %copy-start.7 = (f32[20,72,128]{2,1,0:T(8,128)}, f32[20,72,128]{2,1,0:T(8,128)S(1)}, u32[]{:S(2)}) copy-start(f32[20,72,128]{2,1,0:T(8,128)S(1)} %get-tuple-element.28.e_in) | copy-start | bytes 2211844
  30.7 23.3 %copy-start.4 = (f32[20,72,128]{2,1,0:T(8,128)S(1)}, f32[20,72,128]{2,1,0:T(8,128)}, u32[]{:S(2)}) copy-start(f32[20,72,128]{2,1,0:T(8,128)} %copy-done.3) | copy-start | bytes 2211844
  30.7 23.3 %collective-permute-start.6 = (f32[3,72,128]{2,1,0:T(8,128)S(1)}, f32[3,72,128]{2,1,0:T(8,128)S(1)}, u32[]{:S(2)}, u32[]{:S(2)}) collective-permute-start(f32[3,72,128]{2,1,0:T(8,128)S(1)} %get-tuple-element.30.packed), channel_id=1, source_target_pairs={{0,1},{1,2},{2,3},{3,4},{4,5},{5,6},{6,7},{8,9},{9,10},{10,11},{11... | collective-permute-start | bytes 331784 | tf_op jit(solution)/shard_map/ppermute | solution.py:31
  35.7 18.3 %collective-permute-start.7 = (f32[3,72,128]{2,1,0:T(8,128)S(1)}, f32[3,72,128]{2,1,0:T(8,128)S(1)}, u32[]{:S(2)}, u32[]{:S(2)}) collective-permute-start(f32[3,72,128]{2,1,0:T(8,128)S(1)} %get-tuple-element.30.packed), channel_id=1, source_target_pairs={{1,0},{2,1},{3,2},{4,3},{5,4},{6,5},{7,6},{9,8},{10,9},{11,10},{12... | collective-permute-start | bytes 331784 | tf_op jit(solution)/shard_map/ppermute | solution.py:36
  41.9 4.1 %collective-permute-start = (f32[8,128]{1,0:T(8,128)S(1)}, f32[8,128]{1,0:T(8,128)S(1)}, u32[]{:S(2)}, u32[]{:S(2)}) collective-permute-start(f32[8,128]{1,0:T(8,128)S(1)} %get-tuple-element.20), channel_id=1, source_target_pairs={{0,8},{8,16},{16,24},{1,9},{9,17},{17,25},{2,10},{10,18},{18,26},{... | collective-permute-start | bytes 12296 | tf_op jit(solution)/shard_map/ppermute | solution.py:31
  44.8 4.4 %collective-permute-start.1 = (f32[8,128]{1,0:T(8,128)S(1)}, f32[8,128]{1,0:T(8,128)S(1)}, u32[]{:S(2)}, u32[]{:S(2)}) collective-permute-start(f32[8,128]{1,0:T(8,128)S(1)} %get-tuple-element.21), channel_id=1, source_target_pairs={{8,0},{16,8},{24,16},{9,1},{17,9},{25,17},{10,2},{18,10},{26,18},{... | collective-permute-start | bytes 12296 | tf_op jit(solution)/shard_map/ppermute | solution.py:36
  49.2 26.7 %collective-permute-start.2 = (f32[72,128]{1,0:T(8,128)S(1)}, f32[72,128]{1,0:T(8,128)S(1)}, u32[]{:S(2)}, u32[]{:S(2)}) collective-permute-start(f32[72,128]{1,0:T(8,128)S(1)} %get-tuple-element.23.packed), channel_id=1, source_target_pairs={{0,1},{1,2},{2,3},{3,4},{4,5},{5,6},{6,7},{8,9},{9,10},{10,11},{11... | collective-permute-start | bytes 110600 | tf_op jit(solution)/shard_map/ppermute | solution.py:31
  52.1 23.8 %collective-permute-start.3 = (f32[72,128]{1,0:T(8,128)S(1)}, f32[72,128]{1,0:T(8,128)S(1)}, u32[]{:S(2)}, u32[]{:S(2)}) collective-permute-start(f32[72,128]{1,0:T(8,128)S(1)} %get-tuple-element.23.packed), channel_id=1, source_target_pairs={{1,0},{2,1},{3,2},{4,3},{5,4},{6,5},{7,6},{9,8},{10,9},{11,10},{12... | collective-permute-start | bytes 110600 | tf_op jit(solution)/shard_map/ppermute | solution.py:36
  54.1 1.1 %copy-start.6 = (f32[20,72,128]{2,1,0:T(8,128)S(1)}, f32[20,72,128]{2,1,0:T(8,128)}, u32[]{:S(2)}) copy-start(f32[20,72,128]{2,1,0:T(8,128)} %copy-done.5) | copy-start | bytes 2211844
  55.2 1.1 %copy-start.8 = (f32[20,72,128]{2,1,0:T(8,128)S(1)}, f32[20,72,128]{2,1,0:T(8,128)}, u32[]{:S(2)}) copy-start(f32[20,72,128]{2,1,0:T(8,128)} %copy-done.7) | copy-start | bytes 2211844
